TPU v7x, 256 devices: a whole 4x4x8 slice. The times are simulated.
256 devices in a mesh: frame: 256 (over x, z, y, core).
Axes of the slice: x: 4, y: 4, z: 8, core: 2. Of those that a mesh axis runs over, the one named last changes fastest.
Arguments:
- diag_even: float32 [512, 256, 256], P('frame'), may hold values from -0.375 to 0.375
- inv_odd: float32 [512, 256, 256], P('frame'), as said below
- coupling: float32 [1024, 256, 256], P('frame'), may hold values from -0.375 to 0.375
- arrow_blocks: float32 [1024, 512, 256], P('frame'), as said below
- arrow_tip: float32 [512, 512], P('frame'), may hold values from -6 to 6
Outputs:
- diag_new: float32 [512, 256, 256], P('frame')
- couple_new: float32 [512, 256, 256], P('frame')
- arrow_new: float32 [512, 512, 256], P('frame')
- tip_new: float32 [512, 512], P('frame')
Inputs may be any that keep to these rules, and one draw needn't show every extreme that they name: `inv_odd`: each block is symmetric, with a diagonal near 1 and small off-diagonal entries. `arrow_blocks`: Real-valued entries of order 256 ** -0.5 or smaller.
All inputs are finite; a program needn't handle non-finite values.
Results may differ from a plain program's by a relative error of at most 0.000076.
Values sent between devices are 32-bit elements; how exact they have to be, the bound alone decides.
No kernel may reach another device: no remote copies, remote signals or barrier semaphores. Data moves between devices by JAX's collectives and lax.ppermute only.
A program may use at most 64 MiB of HBM per device.

v0:
```python
import functools

import jax
import jax.numpy as jnp
from jax import lax
from jax.experimental import pallas as pl
from jax.experimental.pallas import tpu as pltpu
from jax.sharding import Mesh
from jax.sharding import PartitionSpec as P

AXES = ("x", "z", "y", "c")
SIZES = (4, 8, 4, 2)
F32 = jnp.float32
NN = (((1,), (0,)), ((), ()))
NT = (((1,), (1,)), ((), ()))
TN = (((0,), (0,)), ((), ()))
HBM = pl.BlockSpec(memory_space=pltpu.HBM)


def halves(x):
    high = x.astype(jnp.bfloat16)
    return high, (x - high.astype(F32)).astype(jnp.bfloat16)


def mul(a, b, dims):
    dot = functools.partial(lax.dot_general, dimension_numbers=dims, preferred_element_type=F32)
    return dot(a[0], b[0]) + (dot(a[0], b[1]) + dot(a[1], b[0]))


def start_all(pairs, sems):
    copies = [pltpu.make_async_copy(src, dst, sems.at[i]) for i, (src, dst) in enumerate(pairs)]
    for copy in copies:
        copy.start()
    return copies


def tip_kernel(inv_ref, arrow_ref, mine_ref, other_ref, p_buf, k_buf, a_buf, sems):
    nx, nz, ny, nc = SIZES
    copies = start_all(
        [pair for h in range(2) for pair in ((inv_ref.at[h], p_buf.at[h]), (arrow_ref.at[2 * h + 1], k_buf.at[h]))],
        sems,
    )
    rows = k_buf.shape[1]
    own = rows // (nx * nz * ny * nc)
    k_split = []
    for h in range(2):
        copies[2 * h].wait()
        copies[2 * h + 1].wait()
        k_split.append(halves(k_buf[h]))
        a = mul(k_split[h], halves(p_buf[h]), NN)
        a_buf[h, 0] = a[:, :128]
        a_buf[h, 1] = a[:, 128:]
    core = lax.axis_index("c")
    for out_ref, part in ((other_ref, 1 - core), (mine_ref, core)):
        total = None
        for h in range(2):
            tiles = []
            for x in range(nx):
                for y in range(ny):
                    for r in range(own):
                        first = ((x * nz * ny + y) * nc + part) * own + r
                        picked = pl.ds(first, nz, stride=ny * nc * own)
                        tiles.append(jnp.concatenate([a_buf[h, 0, picked, :], a_buf[h, 1, picked, :]], axis=1))
            a = halves(jnp.concatenate(tiles, axis=0))
            term = mul(a, k_split[h], NT)
            total = term if total is None else total + term
        out_ref[...] = total


def tip_parts(inv_odd, arrow_blocks):
    _, order, _ = inv_odd.shape
    width = arrow_blocks.shape[1]
    half = jax.ShapeDtypeStruct((width // 2, width), F32)
    return pl.pallas_call(
        tip_kernel,
        name="tip",
        out_shape=(half, half),
        in_specs=[HBM, HBM],
        scratch_shapes=[
            pltpu.VMEM((2, order, order), F32),
            pltpu.VMEM((2, width, order), F32),
            pltpu.VMEM((2, 2, width, order // 2), F32),
            pltpu.SemaphoreType.DMA((4,)),
        ],
        cost_estimate=pl.CostEstimate(flops=1_200_000_000, bytes_accessed=2_600_000, transcendentals=0),
        compiler_params=pltpu.CompilerParams(vmem_limit_bytes=24 << 20),
    )(inv_odd, arrow_blocks)


def right_kernel(inv_ref, link_ref, arrow_ref, sent_ref, p_buf, v_buf, k_buf, sems):
    copies = start_all([(inv_ref.at[1], p_buf), (link_ref.at[3], v_buf), (arrow_ref.at[3], k_buf)], sems)
    copies[0].wait()
    copies[1].wait()
    v = halves(v_buf[...])
    w = halves(mul(halves(p_buf[...]), v, NN))
    order = v_buf.shape[0]
    sent_ref[:order] = mul(v, w, TN)
    copies[2].wait()
    sent_ref[order:] = mul(halves(k_buf[...]), w, NN)


def right_parts(inv_odd, coupling, arrow_blocks):
    _, order, _ = inv_odd.shape
    width = arrow_blocks.shape[1]
    return pl.pallas_call(
        right_kernel,
        name="right",
        out_shape=jax.ShapeDtypeStruct((order + width, order), F32),
        in_specs=[HBM, HBM, HBM],
        scratch_shapes=[
            pltpu.VMEM((order, order), F32),
            pltpu.VMEM((order, order), F32),
            pltpu.VMEM((width, order), F32),
            pltpu.SemaphoreType.DMA((3,)),
        ],
        cost_estimate=pl.CostEstimate(flops=400_000_000, bytes_accessed=1_800_000, transcendentals=0),
        compiler_params=pltpu.CompilerParams(vmem_limit_bytes=24 << 20),
    )(inv_odd, coupling, arrow_blocks)


def rest_kernel(
    even_ref, inv_ref, link_ref, arrow_ref, diag_ref, couple_ref, new_ref,
    e_buf, p_buf, l_buf, k_buf, d_out, c_out, a_out, in_sems, out_sems,
):
    copies = start_all(
        [
            (inv_ref, p_buf),
            (link_ref, l_buf),
            (arrow_ref.at[1], k_buf.at[1]),
            (even_ref, e_buf),
            (arrow_ref.at[0], k_buf.at[0]),
            (arrow_ref.at[3], k_buf.at[3]),
            (arrow_ref.at[2], k_buf.at[2]),
        ],
        in_sems,
    )
    outs = []

    def send(src, dst):
        copy = pltpu.make_async_copy(src, dst, out_sems.at[len(outs)])
        copy.start()
        outs.append(copy)

    copies[0].wait()
    copies[1].wait()
    w = None
    for h in range(2):
        p, u, v = halves(p_buf[h]), halves(l_buf[2 * h]), halves(l_buf[2 * h + 1])
        left = halves(mul(u, p, NN))
        c_out[h] = -mul(left, v, NN)
        send(c_out.at[h], couple_ref.at[h])
        if h == 0:
            copies[2].wait()
            copies[3].wait()
        diag = e_buf[h] - mul(left, u, NT)
        k = halves(k_buf[1]) if h == 0 else None
        if h == 1:
            diag = diag - mul(v0, w, TN)
        d_out[h] = diag
        send(d_out.at[h], diag_ref.at[h])
        if h == 0:
            v0, k0 = v, k
            w = halves(mul(p, v, NN))
            copies[4].wait()
            a_out[0] = k_buf[0] - mul(k, left, NT)
        else:
            copies[5].wait()
            copies[6].wait()
            a_out[1] = k_buf[2] - mul(halves(k_buf[3]), left, NT) - mul(k0, w, NN)
        send(a_out.at[h], new_ref.at[h])
    for copy in outs:
        copy.wait()


def rest_parts(diag_even, inv_odd, coupling, arrow_blocks):
    half, order, _ = inv_odd.shape
    width = arrow_blocks.shape[1]
    square = jax.ShapeDtypeStruct((half, order, order), F32)
    tall = jax.ShapeDtypeStruct((half, width, order), F32)
    return pl.pallas_call(
        rest_kernel,
        name="rest",
        out_shape=(square, square, tall),
        in_specs=[HBM] * 4,
        out_specs=[HBM] * 3,
        scratch_shapes=[
            pltpu.VMEM((half, order, order), F32),
            pltpu.VMEM((half, order, order), F32),
            pltpu.VMEM((2 * half, order, order), F32),
            pltpu.VMEM((2 * half, width, order), F32),
            pltpu.VMEM((half, order, order), F32),
            pltpu.VMEM((half, order, order), F32),
            pltpu.VMEM((half, width, order), F32),
            pltpu.SemaphoreType.DMA((7,)),
            pltpu.SemaphoreType.DMA((6,)),
        ],
        cost_estimate=pl.CostEstimate(flops=1_400_000_000, bytes_accessed=6_000_000, transcendentals=0),
        compiler_params=pltpu.CompilerParams(vmem_limit_bytes=32 << 20),
    )(diag_even, inv_odd, coupling, arrow_blocks)


def settle_kernel(diag_ref, new_ref, got_ref, diag_out, new_out, d_buf, a_buf, g_buf, sems):
    order = d_buf.shape[0]
    copies = start_all([(diag_ref.at[0], d_buf), (got_ref, g_buf), (new_ref.at[0], a_buf)], sems)
    copies[0].wait()
    copies[1].wait()
    d_buf[...] = d_buf[...] - g_buf[:order]
    first = pltpu.make_async_copy(d_buf, diag_out.at[0], sems.at[0])
    first.start()
    copies[2].wait()
    a_buf[...] = a_buf[...] - g_buf[order:]
    second = pltpu.make_async_copy(a_buf, new_out.at[0], sems.at[1])
    second.start()
    first.wait()
    second.wait()


def settle(diag_part, arrow_part, received):
    _, order, _ = diag_part.shape
    width = arrow_part.shape[1]
    return pl.pallas_call(
        settle_kernel,
        name="settle",
        out_shape=(
            jax.ShapeDtypeStruct(diag_part.shape, F32),
            jax.ShapeDtypeStruct(arrow_part.shape, F32),
        ),
        in_specs=[HBM] * 3,
        out_specs=[HBM] * 2,
        input_output_aliases={0: 0, 1: 1},
        scratch_shapes=[
            pltpu.VMEM((order, order), F32),
            pltpu.VMEM((width, order), F32),
            pltpu.VMEM((order + width, order), F32),
            pltpu.SemaphoreType.DMA((3,)),
        ],
        cost_estimate=pl.CostEstimate(flops=200_000, bytes_accessed=2_400_000, transcendentals=0),
        compiler_params=pltpu.CompilerParams(vmem_limit_bytes=16 << 20),
    )(diag_part, arrow_part, received)


def shifted(x, by):
    count = 1
    for size in SIZES:
        count *= size
    pairs = [(i, i + by) for i in range(count) if 0 <= i + by < count]
    return lax.ppermute(x, AXES, pairs)


def per_device(diag_even, inv_odd, coupling, arrow_blocks, arrow_tip):
    own, cols = arrow_tip.shape
    nx, nz, ny, _ = SIZES
    diag_even, inv_odd, coupling, arrow_blocks = (
        pltpu.with_memory_space_constraint(x, pltpu.HBM) for x in (diag_even, inv_odd, coupling, arrow_blocks)
    )
    mine, other = tip_parts(inv_odd, arrow_blocks)
    got = lax.ppermute(other, "c", [(0, 1), (1, 0)])
    sent = right_parts(inv_odd, coupling, arrow_blocks)
    part = (mine + got).reshape(nx * ny, own * nz, cols)
    part = lax.all_to_all(part, ("x", "y"), 0, 0, tiled=True)
    part = part.sum(0)
    received = shifted(sent, 1)
    diag_part, couple_new, arrow_part = rest_parts(diag_even, inv_odd, coupling, arrow_blocks)
    part = part.reshape(own, nz, cols // 128, 128).transpose(1, 2, 0, 3)
    part = part.reshape(nz, own * cols // 128, 128)
    part = lax.all_to_all(part, "z", 0, 0, tiled=True)
    part = part.sum(0)
    part = part.reshape(cols // 128, own, 128).transpose(1, 0, 2)
    tip_new = arrow_tip - part.reshape(own, cols)
    diag_new, arrow_new = settle(diag_part, arrow_part, received)
    return (diag_new, couple_new, arrow_new, tip_new)


def solution(mesh):
    torus = Mesh(mesh.devices.reshape(SIZES), AXES)
    cube = P(AXES, None, None)
    flat = P(AXES, None)

    return jax.shard_map(
        per_device,
        mesh=torus,
        in_specs=(cube, cube, cube, cube, flat),
        out_specs=(cube, cube, cube, flat),
        check_vma=False,
    )
```

profile of v0, /device:TPU:1, one launch (start us, length us, event | category | flops | bytes accessed | tf_op | source)
XLA Modules:
  0.0 47.3 jit_solution(12841658481817013509)
XLA Ops:
  0.6 3.1 %tip.1 = (f32[256,512]{1,0:T(8,128)S(1)}, f32[256,512]{1,0:T(8,128)S(1)}) custom-call(f32[2,256,256]{2,1,0:T(8,128)} %inv_ref.5, f32[4,512,256]{2,1,0:T(8,128)} %arrow_ref.5), custom_call_target="tpu_custom_call" | custom-call | flops 1200000000 | bytes 2600000 | tf_op jit(solution)/shard_map/tip/pallas_call | solution.py:74
  3.8 3.3 %collective-permute-start.1 = (f32[256,512]{1,0:T(8,128)S(1)}, f32[256,512]{1,0:T(8,128)S(1)}, u32[]{:S(2)}, u32[]{:S(2)}) collective-permute-start(f32[256,512]{1,0:T(8,128)S(1)} %get-tuple-element.17), channel_id=1, source_target_pairs={{0,1},{1,0},{2,3},{3,2},{4,5},{5,4},{6,7},{7,6},{8,9},{9,8},{10,11... | collective-permute-start | bytes 1572872 | tf_op jit(solution)/shard_map/ppermute | solution.py:257
  7.1 2.1 %right.1 = f32[768,256]{1,0:T(8,128)S(1)} custom-call(f32[2,256,256]{2,1,0:T(8,128)} %inv_ref.5, f32[4,256,256]{2,1,0:T(8,128)} %link_ref.3, f32[4,512,256]{2,1,0:T(8,128)} %arrow_ref.5), custom_call_target="tpu_custom_call" | custom-call | flops 400000000 | bytes 1800000 | tf_op jit(solution)/shard_map/right/pallas_call | solution.py:105
  9.2 1.9 %collective-permute-start = (f32[768,256]{1,0:T(8,128)S(1)}, f32[768,256]{1,0:T(8,128)S(1)}, u32[]{:S(2)}, u32[]{:S(2)}) collective-permute-start(f32[768,256]{1,0:T(8,128)S(1)} %right.1), channel_id=1, source_target_pairs={{0,1},{1,2},{2,3},{3,4},{4,5},{5,6},{6,7},{7,8},{8,9},{9,10},{10,1... | collective-permute-start | bytes 2359304 | tf_op jit(solution)/shard_map/ppermute | solution.py:247
  11.1 0.0 collective-permute-done.1
  11.1 0.1 add.3
  11.2 24.7 %all_to_all.10 = f32[16,16,512]{2,1,0:T(8,128)S(1)} all-to-all(f32[16,16,512]{2,1,0:T(8,128)S(1)} %bitcast.10), channel_id=1, replica_groups=mesh['x'=4,'z'=8,'y'=4,'c'=2] {'x','y'}, dimensions={0} | all-to-all | bytes 1048576 | tf_op jit(solution)/shard_map/all_to_all | solution.py:260
  35.9 0.6 %copy.13 = f32[8,8,128]{2,1,0:T(8,128)} copy(f32[8,8,128]{2,0,1:T(8,128)S(1)} %bitcast.12) | data formatting | bytes 65536 | tf_op jit(solution)/shard_map/reshape | solution.py:265
  36.6 3.3 %all-to-all-start.1 = ((f32[8,8,128]{2,1,0:T(8,128)}), f32[8,8,128]{2,1,0:T(8,128)S(1)}, u32[]{:S(2)}, u32[]{:S(2)}) async-start(f32[8,8,128]{2,1,0:T(8,128)} %copy.13), calls=%async_computation.1 | async-start | bytes 65536 | tf_op jit(solution)/shard_map/all_to_all | solution.py:266
  39.9 4.7 %rest.1 = (f32[2,256,256]{2,1,0:T(8,128)}, f32[2,256,256]{2,1,0:T(8,128)}, f32[2,512,256]{2,1,0:T(8,128)}) custom-call(f32[2,256,256]{2,1,0:T(8,128)} %even_ref.1, f32[2,256,256]{2,1,0:T(8,128)} %inv_ref.5, f32[4,256,256]{2,1,0:T(8,128)} %link_ref.3, f32[4,512,256]{2,1,0:T(8,128)} %arrow_ref.5), custom_call_target="tpu_custom_call" | custom-call | flops 1400000000 | bytes 6000000 | tf_op jit(solution)/shard_map/rest/pallas_call | solution.py:180
  44.6 0.0 copy-start
  44.7 0.0 collective-permute-done.got_ref
  44.7 2.0 %settle.1 = (f32[2,256,256]{2,1,0:T(8,128)}, f32[2,512,256]{2,1,0:T(8,128)}) custom-call(f32[2,256,256]{2,1,0:T(8,128)} %get-tuple-element.11.diag_ref, f32[2,512,256]{2,1,0:T(8,128)} %get-tuple-element.12.new_ref, f32[768,256]{1,0:T(8,128)S(1)} %collective-permute-done.got_ref), custom_call_target="tpu_custom_call", output_to_operand_aliasing={{0}: (0, {}), {1}: (1, {})} | custom-call | flops 200000 | bytes 2400000 | tf_op jit(solution)/shard_map/settle/pallas_call | solution.py:221
  46.7 0.0 all-to-all-done.1
  46.7 0.0 copy-done
  46.7 0.6 %sub.3 = f32[2,512]{1,0:T(2,128)} subtract(f32[2,512]{1,0:T(2,128)S(1)} %copy-done, f32[2,512]{1,0:T(2,128)S(1)} %bitcast.13) | non-fusion elementwise | flops 1024 | bytes 12288 | tf_op jit(solution)/shard_map/sub | solution.py:269
  (3 shorter events, 0.1 us)
Async XLA Ops:
  3.8 7.3 %collective-permute-start.1 = (f32[256,512]{1,0:T(8,128)S(1)}, f32[256,512]{1,0:T(8,128)S(1)}, u32[]{:S(2)}, u32[]{:S(2)}) collective-permute-start(f32[256,512]{1,0:T(8,128)S(1)} %get-tuple-element.17), channel_id=1, source_target_pairs={{0,1},{1,0},{2,3},{3,2},{4,5},{5,4},{6,7},{7,6},{8,9},{9,8},{10,11... | collective-permute-start | bytes 1572872 | tf_op jit(solution)/shard_map/ppermute | solution.py:257
  9.2 35.5 %collective-permute-start = (f32[768,256]{1,0:T(8,128)S(1)}, f32[768,256]{1,0:T(8,128)S(1)}, u32[]{:S(2)}, u32[]{:S(2)}) collective-permute-start(f32[768,256]{1,0:T(8,128)S(1)} %right.1), channel_id=1, source_target_pairs={{0,1},{1,2},{2,3},{3,4},{4,5},{5,6},{6,7},{7,8},{8,9},{9,10},{10,1... | collective-permute-start | bytes 2359304 | tf_op jit(solution)/shard_map/ppermute | solution.py:247
  36.6 10.1 %all-to-all-start.1 = ((f32[8,8,128]{2,1,0:T(8,128)}), f32[8,8,128]{2,1,0:T(8,128)S(1)}, u32[]{:S(2)}, u32[]{:S(2)}) async-start(f32[8,8,128]{2,1,0:T(8,128)} %copy.13), calls=%async_computation.1 | async-start | bytes 65536 | tf_op jit(solution)/shard_map/all_to_all | solution.py:266
  44.6 2.1 %copy-start = (f32[2,512]{1,0:T(2,128)S(1)}, f32[2,512]{1,0:T(2,128)}, u32[]{:S(2)}) copy-start(f32[2,512]{1,0:T(2,128)} %param.9) | copy-start | bytes 12292
where the time goes:
time: 47.6 us; the launch traced here: 47.3 us
  blocking collectives  24.7 us (52%)
  Pallas kernels  12 us (25%)
  starting transfers between devices  8.54 us (18%)
  between operations  0.74 us (2%)
  other arithmetic  0.73 us (2%)
  local copies, waits for them, and re-layouts  0.63 us (1%)
    all_to_all x1, blocking collectives, per_device(): part = lax.all_to_all(part, ('x', 'y'), 0, 0, tiled=True)  24.7 us
    pallas_call x1, Pallas kernels, rest_parts(): pl.pallas_call(rest_kernel, name='rest', out_shape=(square, square, tall)...  4.74 us
    all_to_all x1, starting transfers between devices, per_device(): part = lax.all_to_all(part, 'z', 0, 0, tiled=True)  3.33 us
    ppermute x1, starting transfers between devices, per_device(): got = lax.ppermute(other, 'c', [(0, 1), (1, 0)])  3.29 us
    pallas_call x1, Pallas kernels, tip_parts(): pl.pallas_call(tip_kernel, name='tip', out_shape=(half, half), in_specs=[...  3.15 us
    pallas_call x1, Pallas kernels, right_parts(): pl.pallas_call(right_kernel, name='right', out_shape=jax.ShapeDtypeStruct...  2.12 us
    pallas_call x1, Pallas kernels, settle(): pl.pallas_call(settle_kernel, name='settle', out_shape=(jax.ShapeDtypeStr...  2.01 us
    ppermute x1, starting transfers between devices, shifted(): return lax.ppermute(x, AXES, pairs)  1.92 us
  transfers between devices with their start and end apart: 3, of which 0 were waited for; matrix products, arithmetic and copies ran while one was open for 2% of the time, Pallas kernels for 19%

commit v1 on v0

v1 whole, which is shorter than its diff:
```python
import functools

import jax
import jax.numpy as jnp
from jax import lax
from jax.experimental import pallas as pl
from jax.experimental.pallas import tpu as pltpu
from jax.sharding import Mesh
from jax.sharding import PartitionSpec as P

AXES = ("x", "z", "y", "c")
SIZES = (4, 8, 4, 2)
F32 = jnp.float32
NN = (((1,), (0,)), ((), ()))
NT = (((1,), (1,)), ((), ()))
TN = (((0,), (0,)), ((), ()))
HBM = pl.BlockSpec(memory_space=pltpu.HBM)


def halves(x):
    high = x.astype(jnp.bfloat16)
    return high, (x - high.astype(F32)).astype(jnp.bfloat16)


def mul(a, b, dims):
    dot = functools.partial(lax.dot_general, dimension_numbers=dims, preferred_element_type=F32)
    return dot(a[0], b[0]) + (dot(a[0], b[1]) + dot(a[1], b[0]))


def start_all(pairs, sems):
    copies = [pltpu.make_async_copy(src, dst, sems.at[i]) for i, (src, dst) in enumerate(pairs)]
    for copy in copies:
        copy.start()
    return copies


def picked_rows(a_buf, h, part):
    nx, nz, ny, nc = SIZES
    own = a_buf.shape[2] // (nx * nz * ny * nc)
    tiles = []
    for x in range(nx):
        for y in range(ny):
            for r in range(own):
                first = ((x * nz * ny + y) * nc + part) * own + r
                rows = pl.ds(first, nz, stride=ny * nc * own)
                tiles.append(jnp.concatenate([a_buf[h, 0, rows, :], a_buf[h, 1, rows, :]], axis=1))
    return halves(jnp.concatenate(tiles, axis=0))


def tip_kernel(inv_ref, arrow_ref, other_ref, a_ref, k_ref, p_buf, k_buf, a_buf, sems):
    copies = start_all(
        [pair for h in range(2) for pair in ((inv_ref.at[h], p_buf.at[h]), (arrow_ref.at[2 * h + 1], k_buf.at[h]))],
        sems,
    )
    core = lax.axis_index("c")
    total = None
    for h in range(2):
        copies[2 * h].wait()
        copies[2 * h + 1].wait()
        k = halves(k_buf[h])
        k_ref[h, 0], k_ref[h, 1] = k
        a = mul(k, halves(p_buf[h]), NN)
        a_buf[h, 0] = a[:, :128]
        a_buf[h, 1] = a[:, 128:]
        term = mul(picked_rows(a_buf, h, 1 - core), k, NT)
        total = term if total is None else total + term
    other_ref[...] = total
    for h in range(2):
        a_ref[h, 0], a_ref[h, 1] = picked_rows(a_buf, h, core)


def tip_parts(inv_odd, arrow_blocks):
    half, order, _ = inv_odd.shape
    width = arrow_blocks.shape[1]
    return pl.pallas_call(
        tip_kernel,
        name="tip",
        out_shape=(
            jax.ShapeDtypeStruct((width // 2, width), F32),
            jax.ShapeDtypeStruct((half, 2, width // 2, order), jnp.bfloat16),
            jax.ShapeDtypeStruct((half, 2, width, order), jnp.bfloat16),
        ),
        in_specs=[HBM, HBM],
        scratch_shapes=[
            pltpu.VMEM((half, order, order), F32),
            pltpu.VMEM((half, width, order), F32),
            pltpu.VMEM((half, 2, width, order // 2), F32),
            pltpu.SemaphoreType.DMA((4,)),
        ],
        cost_estimate=pl.CostEstimate(flops=800_000_000, bytes_accessed=1_600_000, transcendentals=0),
        compiler_params=pltpu.CompilerParams(vmem_limit_bytes=24 << 20),
    )(inv_odd, arrow_blocks)


def mine_kernel(a_ref, k_ref, out_ref):
    terms = [mul((a_ref[h, 0], a_ref[h, 1]), (k_ref[h, 0], k_ref[h, 1]), NT) for h in range(2)]
    out_ref[...] = terms[0] + terms[1]


def mine_part(a_split, k_split):
    return pl.pallas_call(
        mine_kernel,
        name="mine",
        out_shape=jax.ShapeDtypeStruct((a_split.shape[2], k_split.shape[2]), F32),
        cost_estimate=pl.CostEstimate(flops=400_000_000, bytes_accessed=100_000, transcendentals=0),
        compiler_params=pltpu.CompilerParams(vmem_limit_bytes=24 << 20),
    )(a_split, k_split)


def add_kernel(a_ref, b_ref, out_ref):
    out_ref[...] = (a_ref[...] + b_ref[...]).reshape(out_ref.shape)


def added(a, b, shape):
    return pl.pallas_call(
        add_kernel,
        name="added",
        out_shape=jax.ShapeDtypeStruct(shape, F32),
        cost_estimate=pl.CostEstimate(flops=200_000, bytes_accessed=100_000, transcendentals=0),
        compiler_params=pltpu.CompilerParams(vmem_limit_bytes=16 << 20),
    )(a, b)


def fold_kernel(in_ref, out_ref):
    nz, deep, lanes = out_ref.shape
    own = in_ref.shape[1] // nz
    total = in_ref[0]
    for peer in range(1, in_ref.shape[0]):
        total = total + in_ref[peer]
    for block in range(deep // own):
        for r in range(own):
            piece = total[r * nz : (r + 1) * nz, block * lanes : (block + 1) * lanes]
            out_ref[:, block * own + r, :] = piece


def folded(part, own, nz):
    deep = own * part.shape[2] // 128
    return pl.pallas_call(
        fold_kernel,
        name="folded",
        out_shape=jax.ShapeDtypeStruct((nz, deep, 128), F32),
        cost_estimate=pl.CostEstimate(flops=200_000, bytes_accessed=100_000, transcendentals=0),
        compiler_params=pltpu.CompilerParams(vmem_limit_bytes=16 << 20),
    )(part)


def rest_kernel(
    even_ref, inv_ref, link_ref, arrow_ref, diag_ref, couple_ref, new_ref, sent_ref, held_ref,
    e_buf, p_buf, l_buf, k_buf, d_out, c_out, a_out, in_sems, out_sems,
):
    order = p_buf.shape[1]
    copies = start_all(
        [
            (inv_ref, p_buf),
            (link_ref, l_buf),
            (arrow_ref.at[3], k_buf.at[3]),
            (arrow_ref.at[1], k_buf.at[1]),
            (even_ref, e_buf),
            (arrow_ref.at[2], k_buf.at[2]),
            (arrow_ref.at[0], k_buf.at[0]),
        ],
        in_sems,
    )
    outs = []

    def send(src, dst):
        copy = pltpu.make_async_copy(src, dst, out_sems.at[len(outs)])
        copy.start()
        outs.append(copy)

    copies[0].wait()
    copies[1].wait()
    p = [halves(p_buf[h]) for h in range(2)]
    u = [halves(l_buf[2 * h]) for h in range(2)]
    v = [halves(l_buf[2 * h + 1]) for h in range(2)]
    left = []
    for h in range(2):
        left.append(halves(mul(u[h], p[h], NN)))
        c_out[h] = -mul(left[h], v[h], NN)
        send(c_out.at[h], couple_ref.at[h])
    w = [halves(mul(p[h], v[h], NN)) for h in range(2)]
    sent_ref[:order] = mul(v[1], w[1], TN)
    copies[2].wait()
    k = halves(k_buf[3])
    sent_ref[order:] = mul(k, w[1], NN)
    later = mul(k, left[1], NT)
    copies[4].wait()
    d_out[...] = e_buf[1] - mul(left[1], u[1], NT) - mul(v[0], w[0], TN)
    send(d_out, diag_ref.at[1])
    held_ref[:order] = e_buf[0] - mul(left[0], u[0], NT)
    copies[3].wait()
    k = halves(k_buf[1])
    copies[5].wait()
    a_out[...] = k_buf[2] - later - mul(k, w[0], NN)
    send(a_out, new_ref.at[1])
    copies[6].wait()
    held_ref[order:] = k_buf[0] - mul(k, left[0], NT)
    for copy in outs:
        copy.wait()


def rest_parts(diag_even, inv_odd, coupling, arrow_blocks):
    half, order, _ = inv_odd.shape
    width = arrow_blocks.shape[1]
    square = jax.ShapeDtypeStruct((half, order, order), F32)
    tall = jax.ShapeDtypeStruct((half, width, order), F32)
    tower = jax.ShapeDtypeStruct((order + width, order), F32)
    return pl.pallas_call(
        rest_kernel,
        name="rest",
        out_shape=(square, square, tall, tower, tower),
        in_specs=[HBM] * 4,
        out_specs=[HBM] * 3 + [pl.BlockSpec(memory_space=pltpu.VMEM)] * 2,
        scratch_shapes=[
            pltpu.VMEM((half, order, order), F32),
            pltpu.VMEM((half, order, order), F32),
            pltpu.VMEM((2 * half, order, order), F32),
            pltpu.VMEM((2 * half, width, order), F32),
            pltpu.VMEM((order, order), F32),
            pltpu.VMEM((half, order, order), F32),
            pltpu.VMEM((width, order), F32),
            pltpu.SemaphoreType.DMA((7,)),
            pltpu.SemaphoreType.DMA((4,)),
        ],
        cost_estimate=pl.CostEstimate(flops=1_800_000_000, bytes_accessed=6_000_000, transcendentals=0),
        compiler_params=pltpu.CompilerParams(vmem_limit_bytes=32 << 20),
    )(diag_even, inv_odd, coupling, arrow_blocks)


def settle_kernel(diag_ref, new_ref, held_ref, got_ref, diag_out, new_out, buf, sems):
    del diag_ref, new_ref
    order = got_ref.shape[1]
    buf[:order] = held_ref[:order] - got_ref[:order]
    first = pltpu.make_async_copy(buf.at[pl.ds(0, order)], diag_out.at[0], sems.at[0])
    first.start()
    buf[order:] = held_ref[order:] - got_ref[order:]
    second = pltpu.make_async_copy(buf.at[pl.ds(order, buf.shape[0] - order)], new_out.at[0], sems.at[1])
    second.start()
    first.wait()
    second.wait()


def settle(diag_part, arrow_part, held, received):
    return pl.pallas_call(
        settle_kernel,
        name="settle",
        out_shape=(
            jax.ShapeDtypeStruct(diag_part.shape, F32),
            jax.ShapeDtypeStruct(arrow_part.shape, F32),
        ),
        in_specs=[HBM] * 2 + [pl.BlockSpec(memory_space=pltpu.VMEM)] * 2,
        out_specs=[HBM] * 2,
        input_output_aliases={0: 0, 1: 1},
        scratch_shapes=[pltpu.VMEM(held.shape, F32), pltpu.SemaphoreType.DMA((2,))],
        cost_estimate=pl.CostEstimate(flops=200_000, bytes_accessed=1_000_000, transcendentals=0),
        compiler_params=pltpu.CompilerParams(vmem_limit_bytes=16 << 20),
    )(diag_part, arrow_part, held, received)


def shifted(x, by):
    count = 1
    for size in SIZES:
        count *= size
    pairs = [(i, i + by) for i in range(count) if 0 <= i + by < count]
    return lax.ppermute(x, AXES, pairs)


def per_device(diag_even, inv_odd, coupling, arrow_blocks, arrow_tip):
    own, cols = arrow_tip.shape
    nx, nz, ny, _ = SIZES
    diag_even, inv_odd, coupling, arrow_blocks = (
        pltpu.with_memory_space_constraint(x, pltpu.HBM) for x in (diag_even, inv_odd, coupling, arrow_blocks)
    )
    other, a_split, k_split = tip_parts(inv_odd, arrow_blocks)
    got = lax.ppermute(other, "c", [(0, 1), (1, 0)])
    mine = mine_part(a_split, k_split)
    part = added(mine, got, (nx * ny, own * nz, cols))
    part = lax.all_to_all(part, ("x", "y"), 0, 0, tiled=True)
    diag_part, couple_new, arrow_part, sent, held = rest_parts(diag_even, inv_odd, coupling, arrow_blocks)
    received = shifted(sent, 1)
    part = folded(part, own, nz)
    part = lax.all_to_all(part, "z", 0, 0, tiled=True)
    part = part.sum(0)
    part = part.reshape(cols // 128, own, 128).transpose(1, 0, 2)
    tip_new = arrow_tip - part.reshape(own, cols)
    diag_new, arrow_new = settle(diag_part, arrow_part, held, received)
    return (diag_new, couple_new, arrow_new, tip_new)


def solution(mesh):
    torus = Mesh(mesh.devices.reshape(SIZES), AXES)
    cube = P(AXES, None, None)
    flat = P(AXES, None)

    return jax.shard_map(
        per_device,
        mesh=torus,
        in_specs=(cube, cube, cube, cube, flat),
        out_specs=(cube, cube, cube, flat),
        check_vma=False,
    )
```

time: 47.6 us -> 51.2 us (1.076)
  waiting for transfers between devices: 0.01 us -> 5.85 us
  Pallas kernels: 12 us -> 11.2 us
  local copies, waits for them, and re-layouts: 0.63 us -> 0.01 us
  blocking collectives: 24.7 us -> 24.1 us
    all_to_all x1, waiting for transfers between devices: 0.01 us -> 5.85 us  [per_device(): part = lax.all_to_all(part, 'z', 0, 0, tiled=True)]
    pallas_call x1, Pallas kernels: 2.01 us -> 0.93 us  [settle(): pl.pallas_call(settle_kernel, name='settle', out_shape=(jax.ShapeDtypeStr...]
    reshape x1 -> x0, local copies, waits for them, and re-layouts: 0.62 us -> none  [per_device(): part = part.reshape(nz, own * cols // 128, 128)]
    all_to_all x1, blocking collectives: 24.7 us -> 24.1 us  [per_device(): part = lax.all_to_all(part, ('x', 'y'), 0, 0, tiled=True)]
    pallas_call x3 -> x5, Pallas kernels: 10 us -> 10.2 us  [the longest x1 5.47 us: rest_parts(): pl.pallas_call(rest_kernel, name='rest', out_shape=(square, square, tall,...]
  transfers between devices with their start and end apart: 3 -> 3, of which waited for: 0 -> 1; matrix products, arithmetic and copies ran while one was open for 2% -> 0% of each run, Pallas kernels for 19% -> 15%
where the time goes in v1:
time: 51.2 us; the launch traced here: 51 us
  blocking collectives  24.1 us (47%)
  Pallas kernels  11.2 us (22%)
  starting transfers between devices  8.54 us (17%)
  waiting for transfers between devices  5.85 us (11%)
  between operations  0.7 us (1%)
  other arithmetic  0.61 us (1%)
    all_to_all x1, blocking collectives, per_device(): part = lax.all_to_all(part, ('x', 'y'), 0, 0, tiled=True)  24.1 us
    all_to_all x1, waiting for transfers between devices, per_device(): part = lax.all_to_all(part, 'z', 0, 0, tiled=True)  5.85 us
    pallas_call x1, Pallas kernels, rest_parts(): pl.pallas_call(rest_kernel, name='rest', out_shape=(square, square, tall,...  5.47 us
    pallas_call x1, Pallas kernels, tip_parts(): pl.pallas_call(tip_kernel, name='tip', out_shape=(jax.ShapeDtypeStruct((w...  3.47 us
    all_to_all x1, starting transfers between devices, per_device(): part = lax.all_to_all(part, 'z', 0, 0, tiled=True)  3.34 us
    ppermute x1, starting transfers between devices, per_device(): got = lax.ppermute(other, 'c', [(0, 1), (1, 0)])  3.29 us
    ppermute x1, starting transfers between devices, shifted(): return lax.ppermute(x, AXES, pairs)  1.92 us
  transfers between devices with their start and end apart: 3, of which 1 were waited for; matrix products, arithmetic and copies ran while one was open for 0% of the time, Pallas kernels for 15%

profile of v1, /device:TPU:1, one launch (start us, length us, event | category | flops | bytes accessed | tf_op | source)
XLA Modules:
  0.0 51.0 jit_solution(4801662518984713282)
XLA Ops:
  0.6 3.5 %tip.1 = (f32[256,512]{1,0:T(8,128)S(1)}, bf16[2,2,256,256]{3,2,1,0:T(8,128)(2,1)S(1)}, bf16[2,2,512,256]{3,2,1,0:T(8,128)(2,1)S(1)}) custom-call(f32[2,256,256]{2,1,0:T(8,128)} %inv_ref.3, f32[4,512,256]{2,1,0:T(8,128)} %arrow_ref.3), custom_call_target="tpu_custom_call" | custom-call | flops 800000000 | bytes 1600000 | tf_op jit(solution)/shard_map/tip/pallas_call | solution.py:75
  4.1 3.3 %collective-permute-start.1 = (f32[256,512]{1,0:T(8,128)S(1)}, f32[256,512]{1,0:T(8,128)S(1)}, u32[]{:S(2)}, u32[]{:S(2)}) collective-permute-start(f32[256,512]{1,0:T(8,128)S(1)} %get-tuple-element.23), channel_id=1, source_target_pairs={{0,1},{1,0},{2,3},{3,2},{4,5},{5,4},{6,7},{7,6},{8,9},{9,8},{10,11... | collective-permute-start | bytes 1572872 | tf_op jit(solution)/shard_map/ppermute | solution.py:275
  7.4 5.5 %rest.1 = (f32[2,256,256]{2,1,0:T(8,128)}, f32[2,256,256]{2,1,0:T(8,128)}, f32[2,512,256]{2,1,0:T(8,128)}, f32[768,256]{1,0:T(8,128)S(1)}, f32[768,256]{1,0:T(8,128)S(1)}) custom-call(f32[2,256,256]{2,1,0:T(8,128)} %even_ref.1, f32[2,256,256]{2,1,0:T(8,128)} %inv_ref.3, f32[4,256,256]{2,1,0:T(8,128)} %link_ref.1, f32[4,512,256]{2,1,0:T(8,128)} %arrow_ref.3), custom_call_target="tpu_custom_call" | custom-call | flops 1800000000 | bytes 6000000 | tf_op jit(solution)/shard_map/rest/pallas_call | solution.py:208
  12.9 1.9 %collective-permute-start = (f32[768,256]{1,0:T(8,128)S(1)}, f32[768,256]{1,0:T(8,128)S(1)}, u32[]{:S(2)}, u32[]{:S(2)}) collective-permute-start(f32[768,256]{1,0:T(8,128)S(1)} %get-tuple-element.17), channel_id=1, source_target_pairs={{0,1},{1,2},{2,3},{3,4},{4,5},{5,6},{6,7},{7,8},{8,9},{9,10},{10,1... | collective-permute-start | bytes 2359304 | tf_op jit(solution)/shard_map/ppermute | solution.py:265
  14.8 0.6 %mine.1.a_ref = f32[256,512]{1,0:T(8,128)S(1)} custom-call(bf16[2,2,256,256]{3,2,1,0:T(8,128)(2,1)S(1)} %get-tuple-element.21.a_ref, bf16[2,2,512,256]{3,2,1,0:T(8,128)(2,1)S(1)} %get-tuple-element.22.k_ref), custom_call_target="tpu_custom_call" | custom-call | flops 400000000 | bytes 100000 | tf_op jit(solution)/shard_map/mine/pallas_call | solution.py:101
  15.4 0.0 collective-permute-done.1.b_ref
  15.4 0.1 added.1
  15.5 24.1 %all_to_all.10.in_ref = f32[16,16,512]{2,1,0:T(8,128)S(1)} all-to-all(f32[16,16,512]{2,1,0:T(8,128)S(1)} %added.1), channel_id=1, replica_groups=mesh['x'=4,'z'=8,'y'=4,'c'=2] {'x','y'}, dimensions={0} | all-to-all | bytes 1048576 | tf_op jit(solution)/shard_map/all_to_all | solution.py:278
  39.6 0.0 copy-start
  39.6 0.7 %folded.1 = f32[8,8,128]{2,1,0:T(8,128)} custom-call(f32[16,16,512]{2,1,0:T(8,128)S(1)} %all_to_all.10.in_ref), custom_call_target="tpu_custom_call" | custom-call | flops 200000 | bytes 100000 | tf_op jit(solution)/shard_map/folded/pallas_call | solution.py:138
  40.2 3.3 %all-to-all-start.1 = ((f32[8,8,128]{2,1,0:T(8,128)}), f32[8,8,128]{2,1,0:T(8,128)S(1)}, u32[]{:S(2)}, u32[]{:S(2)}) async-start(f32[8,8,128]{2,1,0:T(8,128)} %folded.1), calls=%async_computation.1 | async-start | bytes 65536 | tf_op jit(solution)/shard_map/all_to_all | solution.py:282
  43.6 0.0 collective-permute-done.got_ref
  43.6 0.9 %settle.1 = (f32[2,256,256]{2,1,0:T(8,128)}, f32[2,512,256]{2,1,0:T(8,128)}) custom-call(f32[2,256,256]{2,1,0:T(8,128)} %get-tuple-element.14.diag_ref, f32[2,512,256]{2,1,0:T(8,128)} %get-tuple-element.15.new_ref, f32[768,256]{1,0:T(8,128)S(1)} %get-tuple-element.16.held_ref, ...), custom_call_target="tpu_custom_call", output_to_operand_aliasing={{0}: (0, {}), {1}: (1, {})} | custom-call | flops 200000 | bytes 1000000 | tf_op jit(solution)/shard_map/settle/pallas_call | solution.py:244
  44.5 5.8 %all-to-all-done.1 = f32[8,8,128]{2,1,0:T(8,128)S(1)} async-done(((f32[8,8,128]{2,1,0:T(8,128)}), f32[8,8,128]{2,1,0:T(8,128)S(1)}, u32[]{:S(2)}, u32[]{:S(2)}) %all-to-all-start.1) | async-done | bytes 32800 | tf_op jit(solution)/shard_map/all_to_all | solution.py:282
  50.4 0.0 copy-done
  50.4 0.6 %sub.3 = f32[2,512]{1,0:T(2,128)} subtract(f32[2,512]{1,0:T(2,128)S(1)} %copy-done, f32[2,512]{1,0:T(2,128)S(1)} %bitcast.5) | non-fusion elementwise | flops 1024 | bytes 12288 | tf_op jit(solution)/shard_map/sub | solution.py:285
  (1 shorter events, 0.0 us)
Async XLA Ops:
  4.1 11.3 %collective-permute-start.1 = (f32[256,512]{1,0:T(8,128)S(1)}, f32[256,512]{1,0:T(8,128)S(1)}, u32[]{:S(2)}, u32[]{:S(2)}) collective-permute-start(f32[256,512]{1,0:T(8,128)S(1)} %get-tuple-element.23), channel_id=1, source_target_pairs={{0,1},{1,0},{2,3},{3,2},{4,5},{5,4},{6,7},{7,6},{8,9},{9,8},{10,11... | collective-permute-start | bytes 1572872 | tf_op jit(solution)/shard_map/ppermute | solution.py:275
  12.9 30.7 %collective-permute-start = (f32[768,256]{1,0:T(8,128)S(1)}, f32[768,256]{1,0:T(8,128)S(1)}, u32[]{:S(2)}, u32[]{:S(2)}) collective-permute-start(f32[768,256]{1,0:T(8,128)S(1)} %get-tuple-element.17), channel_id=1, source_target_pairs={{0,1},{1,2},{2,3},{3,4},{4,5},{5,6},{6,7},{7,8},{8,9},{9,10},{10,1... | collective-permute-start | bytes 2359304 | tf_op jit(solution)/shard_map/ppermute | solution.py:265
  39.6 10.8 %copy-start = (f32[2,512]{1,0:T(2,128)S(1)}, f32[2,512]{1,0:T(2,128)}, u32[]{:S(2)}) copy-start(f32[2,512]{1,0:T(2,128)} %param.9) | copy-start | bytes 12292
  40.2 10.1 %all-to-all-start.1 = ((f32[8,8,128]{2,1,0:T(8,128)}), f32[8,8,128]{2,1,0:T(8,128)S(1)}, u32[]{:S(2)}, u32[]{:S(2)}) async-start(f32[8,8,128]{2,1,0:T(8,128)} %folded.1), calls=%async_computation.1 | async-start | bytes 65536 | tf_op jit(solution)/shard_map/all_to_all | solution.py:282

commit v2 on v1

v2 whole, which is shorter than its diff:
```python
import functools

import jax
import jax.numpy as jnp
from jax import lax
from jax.experimental import pallas as pl
from jax.experimental.pallas import tpu as pltpu
from jax.sharding import Mesh
from jax.sharding import PartitionSpec as P

AXES = ("x", "z", "y", "c")
SIZES = (4, 8, 4, 2)
PLANE = (
    (7, 1, 15, 6, 13, 4, 3, 5, 0, 8, 12, 11, 10, 9, 14, 2),
    (10, 15, 8, 3, 5, 14, 4, 9, 13, 1, 0, 2, 7, 6, 11, 12),
)
COLUMN = (4, 0, 2, 6, 1, 5, 3, 7)
F32 = jnp.float32
NN = (((1,), (0,)), ((), ()))
NT = (((1,), (1,)), ((), ()))
TN = (((0,), (0,)), ((), ()))
HBM = pl.BlockSpec(memory_space=pltpu.HBM)


def halves(x):
    high = x.astype(jnp.bfloat16)
    return high, (x - high.astype(F32)).astype(jnp.bfloat16)


def mul(a, b, dims):
    dot = functools.partial(lax.dot_general, dimension_numbers=dims, preferred_element_type=F32)
    return dot(a[0], b[0]) + (dot(a[0], b[1]) + dot(a[1], b[0]))


def start_all(pairs, sems):
    copies = [pltpu.make_async_copy(src, dst, sems.at[i]) for i, (src, dst) in enumerate(pairs)]
    for copy in copies:
        copy.start()
    return copies


def picked_rows(a_buf, h, part):
    nx, nz, ny, nc = SIZES
    own = a_buf.shape[2] // (nx * nz * ny * nc)
    tiles = []
    for chips in zip(*PLANE, strict=True):
        starts = [(chip // ny * nz * ny + chip % ny) * nc * own for chip in chips]
        start = jnp.where(part == 0, starts[0], starts[1]) + part * own
        for r in range(own):
            rows = pl.ds(start + r, nz, stride=ny * nc * own)
            tiles.append(jnp.concatenate([a_buf[h, 0, rows, :], a_buf[h, 1, rows, :]], axis=1))
    return halves(jnp.concatenate(tiles, axis=0))


def tip_kernel(inv_ref, arrow_ref, other_ref, a_ref, k_ref, p_ref, sems):
    copies = start_all(
        [pair for h in range(2) for pair in ((inv_ref.at[h], p_ref.at[h]), (arrow_ref.at[2 * h + 1], k_ref.at[h]))],
        sems,
    )
    core = lax.axis_index("c")
    total = None
    for h in range(2):
        copies[2 * h].wait()
        copies[2 * h + 1].wait()
        k = halves(k_ref[h])
        a = mul(k, halves(p_ref[h]), NN)
        a_ref[h, 0] = a[:, :128]
        a_ref[h, 1] = a[:, 128:]
        term = mul(picked_rows(a_ref, h, 1 - core), k, NT)
        total = term if total is None else total + term
    other_ref[...] = total


def tip_parts(inv_odd, arrow_blocks):
    half, order, _ = inv_odd.shape
    width = arrow_blocks.shape[1]
    return pl.pallas_call(
        tip_kernel,
        name="tip",
        out_shape=(
            jax.ShapeDtypeStruct((width // 2, width), F32),
            jax.ShapeDtypeStruct((half, 2, width, order // 2), F32),
            jax.ShapeDtypeStruct((half, width, order), F32),
            jax.ShapeDtypeStruct((half, order, order), F32),
        ),
        in_specs=[HBM, HBM],
        scratch_shapes=[pltpu.SemaphoreType.DMA((4,))],
        cost_estimate=pl.CostEstimate(flops=800_000_000, bytes_accessed=1_600_000, transcendentals=0),
        compiler_params=pltpu.CompilerParams(vmem_limit_bytes=24 << 20),
    )(inv_odd, arrow_blocks)


def mine_kernel(a_ref, k_ref, p_ref, link_ref, out_ref, sent_ref, v_buf, sem):
    copy = pltpu.make_async_copy(link_ref.at[3], v_buf, sem)
    copy.start()
    core = lax.axis_index("c")
    k = [halves(k_ref[h]) for h in range(2)]
    out_ref[...] = mul(picked_rows(a_ref, 0, core), k[0], NT) + mul(picked_rows(a_ref, 1, core), k[1], NT)
    copy.wait()
    order = v_buf.shape[0]
    v = halves(v_buf[...])
    w = halves(mul(halves(p_ref[1]), v, NN))
    sent_ref[:order] = mul(v, w, TN)
    sent_ref[order:] = mul(k[1], w, NN)


def mine_part(a, k, p, coupling):
    _, width, order = k.shape
    vmem = pl.BlockSpec(memory_space=pltpu.VMEM)
    return pl.pallas_call(
        mine_kernel,
        name="mine",
        out_shape=(
            jax.ShapeDtypeStruct((width // 2, width), F32),
            jax.ShapeDtypeStruct((order + width, order), F32),
        ),
        in_specs=[vmem, vmem, vmem, HBM],
        scratch_shapes=[pltpu.VMEM((order, order), F32), pltpu.SemaphoreType.DMA(())],
        cost_estimate=pl.CostEstimate(flops=800_000_000, bytes_accessed=300_000, transcendentals=0),
        compiler_params=pltpu.CompilerParams(vmem_limit_bytes=24 << 20),
    )(a, k, p, coupling)


def add_kernel(a_ref, b_ref, out_ref, buf, sems):
    pieces = sems.shape[0]
    rows = a_ref.shape[0] // pieces
    copies = []
    for i in range(pieces):
        part = slice(i * rows, (i + 1) * rows)
        major = pl.ds(i * buf.shape[0] // pieces, buf.shape[0] // pieces)
        buf[major] = (a_ref[part] + b_ref[part]).reshape(buf.shape[0] // pieces, *buf.shape[1:])
        copies.append(pltpu.make_async_copy(buf.at[major], out_ref.at[major], sems.at[i]))
        copies[-1].start()
    for copy in copies:
        copy.wait()


def added(a, b, shape):
    return pl.pallas_call(
        add_kernel,
        name="added",
        out_shape=jax.ShapeDtypeStruct(shape, F32),
        out_specs=HBM,
        scratch_shapes=[pltpu.VMEM(shape, F32), pltpu.SemaphoreType.DMA((4,))],
        cost_estimate=pl.CostEstimate(flops=200_000, bytes_accessed=100_000, transcendentals=0),
        compiler_params=pltpu.CompilerParams(vmem_limit_bytes=16 << 20),
    )(a, b)


def fold_kernel(in_ref, out_ref):
    nz, deep, lanes = out_ref.shape
    own = in_ref.shape[1] // nz
    total = in_ref[0]
    for peer in range(1, in_ref.shape[0]):
        total = total + in_ref[peer]
    for block in range(deep // own):
        for r in range(own):
            for k, z in enumerate(COLUMN):
                row = slice(r * nz + z, r * nz + z + 1)
                out_ref[k, block * own + r : block * own + r + 1, :] = total[row, block * lanes : (block + 1) * lanes]


def folded(part, own, nz):
    deep = own * part.shape[2] // 128
    return pl.pallas_call(
        fold_kernel,
        name="folded",
        out_shape=jax.ShapeDtypeStruct((nz, deep, 128), F32),
        cost_estimate=pl.CostEstimate(flops=200_000, bytes_accessed=100_000, transcendentals=0),
        compiler_params=pltpu.CompilerParams(vmem_limit_bytes=16 << 20),
    )(part)


def final_kernel(in_ref, tip_ref, out_ref):
    total = in_ref[0]
    for peer in range(1, in_ref.shape[0]):
        total = total + in_ref[peer]
    own, cols = out_ref.shape
    for block in range(cols // 128):
        lanes = slice(block * 128, (block + 1) * 128)
        out_ref[:, lanes] = tip_ref[:, lanes] - total[block * own : (block + 1) * own]


def final(part, arrow_tip):
    return pl.pallas_call(
        final_kernel,
        name="final",
        out_shape=jax.ShapeDtypeStruct(arrow_tip.shape, F32),
        cost_estimate=pl.CostEstimate(flops=10_000, bytes_accessed=40_000, transcendentals=0),
        compiler_params=pltpu.CompilerParams(vmem_limit_bytes=16 << 20),
    )(part, arrow_tip)


def send(src, dst, sem):
    copy = pltpu.make_async_copy(src, dst, sem)
    copy.start()
    return copy


def square_kernel(
    even_ref, inv_ref, link_ref, diag_ref, couple_ref, held_ref, left_ref, w_ref,
    e_buf, p_buf, l_buf, d_out, c_out, in_sems, out_sems,
):
    copies = start_all(
        [(inv_ref.at[0], p_buf.at[0]), (link_ref.at[pl.ds(0, 2)], l_buf.at[pl.ds(0, 2)])]
        + [(inv_ref.at[1], p_buf.at[1]), (link_ref.at[pl.ds(2, 2)], l_buf.at[pl.ds(2, 2)]), (even_ref, e_buf)],
        in_sems,
    )
    outs = []
    left, u, v = [], [], []
    for h in range(2):
        copies[2 * h].wait()
        copies[2 * h + 1].wait()
        p = halves(p_buf[h])
        u.append(halves(l_buf[2 * h]))
        v.append(halves(l_buf[2 * h + 1]))
        left.append(halves(mul(u[h], p, NN)))
        left_ref[h, 0], left_ref[h, 1] = left[h]
        c_out[h] = -mul(left[h], v[h], NN)
        outs.append(send(c_out.at[h], couple_ref.at[h], out_sems.at[h]))
        if h == 0:
            w = halves(mul(p, v[0], NN))
            w_ref[0], w_ref[1] = w
    copies[4].wait()
    d_out[...] = e_buf[1] - mul(left[1], u[1], NT) - mul(v[0], w, TN)
    outs.append(send(d_out, diag_ref.at[1], out_sems.at[2]))
    held_ref[...] = e_buf[0] - mul(left[0], u[0], NT)
    for copy in outs:
        copy.wait()


def square_parts(diag_even, inv_odd, coupling):
    half, order, _ = inv_odd.shape
    vmem = pl.BlockSpec(memory_space=pltpu.VMEM)
    blocks = jax.ShapeDtypeStruct((half, order, order), F32)
    pair = pltpu.VMEM((half, order, order), F32)
    return pl.pallas_call(
        square_kernel,
        name="square",
        out_shape=(
            blocks,
            blocks,
            jax.ShapeDtypeStruct((order, order), F32),
            jax.ShapeDtypeStruct((half, 2, order, order), jnp.bfloat16),
            jax.ShapeDtypeStruct((2, order, order), jnp.bfloat16),
        ),
        in_specs=[HBM] * 3,
        out_specs=[HBM, HBM, vmem, vmem, vmem],
        scratch_shapes=[
            pair,
            pair,
            pltpu.VMEM((2 * half, order, order), F32),
            pltpu.VMEM((order, order), F32),
            pair,
            pltpu.SemaphoreType.DMA((5,)),
            pltpu.SemaphoreType.DMA((3,)),
        ],
        cost_estimate=pl.CostEstimate(flops=800_000_000, bytes_accessed=2_700_000, transcendentals=0),
        compiler_params=pltpu.CompilerParams(vmem_limit_bytes=24 << 20),
    )(diag_even, inv_odd, coupling)


def tall_kernel(arrow_ref, left_ref, w_ref, new_ref, held_ref, k_buf, a_out, in_sems, out_sem):
    frames = (3, 1, 2, 0)
    copies = start_all([(arrow_ref.at[i], k_buf.at[i]) for i in frames], in_sems)
    copies[0].wait()
    later = mul(halves(k_buf[3]), (left_ref[1, 0], left_ref[1, 1]), NT)
    copies[1].wait()
    k = halves(k_buf[1])
    later = later + mul(k, (w_ref[0], w_ref[1]), NN)
    copies[2].wait()
    a_out[...] = k_buf[2] - later
    out = send(a_out, new_ref.at[1], out_sem)
    copies[3].wait()
    held_ref[...] = k_buf[0] - mul(k, (left_ref[0, 0], left_ref[0, 1]), NT)
    out.wait()


def tall_parts(arrow_blocks, left, w):
    frames, width, order = arrow_blocks.shape
    vmem = pl.BlockSpec(memory_space=pltpu.VMEM)
    return pl.pallas_call(
        tall_kernel,
        name="tall",
        out_shape=(
            jax.ShapeDtypeStruct((frames // 2, width, order), F32),
            jax.ShapeDtypeStruct((width, order), F32),
        ),
        in_specs=[HBM, vmem, vmem],
        out_specs=[HBM, vmem],
        scratch_shapes=[
            pltpu.VMEM((frames, width, order), F32),
            pltpu.VMEM((width, order), F32),
            pltpu.SemaphoreType.DMA((4,)),
            pltpu.SemaphoreType.DMA(()),
        ],
        cost_estimate=pl.CostEstimate(flops=600_000_000, bytes_accessed=2_600_000, transcendentals=0),
        compiler_params=pltpu.CompilerParams(vmem_limit_bytes=24 << 20),
    )(arrow_blocks, left, w)


def settle_kernel(diag_ref, new_ref, square_ref, tall_ref, got_ref, diag_out, new_out, d_buf, a_buf, sems):
    del diag_ref, new_ref
    order = got_ref.shape[1]
    d_buf[...] = square_ref[...] - got_ref[:order]
    first = send(d_buf, diag_out.at[0], sems.at[0])
    a_buf[...] = tall_ref[...] - got_ref[order:]
    second = send(a_buf, new_out.at[0], sems.at[1])
    first.wait()
    second.wait()


def settle(diag_part, arrow_part, square, tall, received):
    return pl.pallas_call(
        settle_kernel,
        name="settle",
        out_shape=(
            jax.ShapeDtypeStruct(diag_part.shape, F32),
            jax.ShapeDtypeStruct(arrow_part.shape, F32),
        ),
        in_specs=[HBM] * 2 + [pl.BlockSpec(memory_space=pltpu.VMEM)] * 3,
        out_specs=[HBM] * 2,
        input_output_aliases={0: 0, 1: 1},
        scratch_shapes=[
            pltpu.VMEM(square.shape, F32),
            pltpu.VMEM(tall.shape, F32),
            pltpu.SemaphoreType.DMA((2,)),
        ],
        cost_estimate=pl.CostEstimate(flops=200_000, bytes_accessed=1_000_000, transcendentals=0),
        compiler_params=pltpu.CompilerParams(vmem_limit_bytes=16 << 20),
    )(diag_part, arrow_part, square, tall, received)


def place(x, z, y, core):
    _, nz, ny, nc = SIZES
    return ((x * nz + z) * ny + y) * nc + core


def plane_groups():
    _, nz, ny, nc = SIZES
    return [[place(chip // ny, z, chip % ny, core) for chip in PLANE[core]] for z in range(nz) for core in range(nc)]


def column_groups():
    nx, _, ny, nc = SIZES
    return [[place(x, z, y, core) for z in COLUMN] for x in range(nx) for y in range(ny) for core in range(nc)]


def shifted(x, by):
    count = 1
    for size in SIZES:
        count *= size
    pairs = [(i, i + by) for i in range(count) if 0 <= i + by < count]
    return lax.ppermute(x, AXES, pairs)


def per_device(diag_even, inv_odd, coupling, arrow_blocks, arrow_tip):
    own, cols = arrow_tip.shape
    nx, nz, ny, _ = SIZES
    diag_even, inv_odd, coupling, arrow_blocks = (
        pltpu.with_memory_space_constraint(x, pltpu.HBM) for x in (diag_even, inv_odd, coupling, arrow_blocks)
    )
    other, a_kept, k_kept, p_kept = tip_parts(inv_odd, arrow_blocks)
    got = lax.ppermute(other, "c", [(0, 1), (1, 0)])
    mine, sent = mine_part(a_kept, k_kept, p_kept, coupling)
    part = added(mine, got, (nx * ny, own * nz, cols))
    part = lax.all_to_all(part, AXES, 0, 0, axis_index_groups=plane_groups(), tiled=True)
    diag_part, couple_new, square, left, w = square_parts(diag_even, inv_odd, coupling)
    received = shifted(sent, 1)
    arrow_part, tall = tall_parts(arrow_blocks, left, w)
    part = folded(part, own, nz)
    part = lax.all_to_all(part, AXES, 0, 0, axis_index_groups=column_groups(), tiled=True)
    tip_new = final(part, arrow_tip)
    diag_new, arrow_new = settle(diag_part, arrow_part, square, tall, received)
    return (diag_new, couple_new, arrow_new, tip_new)


def solution(mesh):
    torus = Mesh(mesh.devices.reshape(SIZES), AXES)
    cube = P(AXES, None, None)
    flat = P(AXES, None)

    return jax.shard_map(
        per_device,
        mesh=torus,
        in_specs=(cube, cube, cube, cube, flat),
        out_specs=(cube, cube, cube, flat),
        check_vma=False,
    )
```

time: 51.2 us -> 51.2 us (level)
  the two profiles are of different devices: /device:TPU:1 before, /device:TPU:32 now
where the time goes in v2:
time: 51.2 us; the launch traced here: 50.9 us
  starting transfers between devices  18 us (35%)
  blocking collectives  17.4 us (34%)
  Pallas kernels  14.7 us (29%)
  between operations  0.73 us (1%)
    all_to_all x1, blocking collectives, per_device(): lax.all_to_all(part, AXES, 0, 0, axis_index_groups=plane_groups(), tiled=...  17.4 us
    all_to_all x1, starting transfers between devices, per_device(): lax.all_to_all(part, AXES, 0, 0, axis_index_groups=column_groups(), tiled...  15.5 us
    pallas_call x1, Pallas kernels, square_parts(): pl.pallas_call(square_kernel, name='square', out_shape=(blocks, blocks, j...  3.52 us
    pallas_call x1, Pallas kernels, tip_parts(): pl.pallas_call(tip_kernel, name='tip', out_shape=(jax.ShapeDtypeStruct((w...  3.26 us
    pallas_call x1, Pallas kernels, tall_parts(): pl.pallas_call(tall_kernel, name='tall', out_shape=(jax.ShapeDtypeStruct(...  2.87 us
    ppermute x1, starting transfers between devices, shifted(): return lax.ppermute(x, AXES, pairs)  2.4 us
    pallas_call x1, Pallas kernels, mine_part(): pl.pallas_call(mine_kernel, name='mine', out_shape=(jax.ShapeDtypeStruct(...  2.07 us
  transfers between devices with their start and end apart: 3, of which 0 were waited for; matrix products, arithmetic and copies ran while one was open for 0% of the time, Pallas kernels for 21%

profile of v2, /device:TPU:32, one launch (start us, length us, event | category | flops | bytes accessed | tf_op | source)
XLA Modules:
  0.0 50.9 jit_solution(13708888174905549588)
XLA Ops:
  0.6 3.3 %tip.1 = (f32[256,512]{1,0:T(8,128)S(1)}, f32[2,2,512,128]{3,2,1,0:T(8,128)S(1)}, f32[2,512,256]{2,1,0:T(8,128)S(1)}, f32[2,256,256]{2,1,0:T(8,128)S(1)}) custom-call(f32[2,256,256]{2,1,0:T(8,128)} %inv_ref.3, f32[4,512,256]{2,1,0:T(8,128)} %arrow_ref.3), custom_call_target="tpu_custom_call" | custom-call | flops 800000000 | bytes 1600000 | tf_op jit(solution)/shard_map/tip/pallas_call | solution.py:77
  3.9 0.1 collective-permute-start.1
  4.0 2.1 %mine.1 = (f32[256,512]{1,0:T(8,128)S(1)}, f32[768,256]{1,0:T(8,128)S(1)}) custom-call(f32[2,2,512,128]{3,2,1,0:T(8,128)S(1)} %get-tuple-element.25.a_ref, f32[2,512,256]{2,1,0:T(8,128)S(1)} %get-tuple-element.26.k_ref, f32[2,256,256]{2,1,0:T(8,128)S(1)} %get-tuple-element.27.p_ref, f32[4,256,256]{2,1,0:T(8,128)} %link_ref.3), custom_call_target="tpu_custom_call" | custom-call | flops 800000000 | bytes 300000 | tf_op jit(solution)/shard_map/mine/pallas_call | solution.py:110
  6.1 2.4 %collective-permute-start = (f32[768,256]{1,0:T(8,128)S(1)}, f32[768,256]{1,0:T(8,128)S(1)}, u32[]{:S(2)}, u32[]{:S(2)}) collective-permute-start(f32[768,256]{1,0:T(8,128)S(1)} %get-tuple-element.28), channel_id=1, source_target_pairs={{0,1},{1,2},{2,3},{3,4},{4,5},{5,6},{6,7},{7,8},{8,9},{9,10},{10,1... | collective-permute-start | bytes 2359304 | tf_op jit(solution)/shard_map/ppermute | solution.py:354
  8.5 0.0 collective-permute-done.1.b_ref
  8.5 0.8 %added.1 = f32[16,16,512]{2,1,0:T(8,128)S(1)} custom-call(f32[256,512]{1,0:T(8,128)S(1)} %get-tuple-element.32.a_ref, f32[256,512]{1,0:T(8,128)S(1)} %collective-permute-done.1.b_ref), custom_call_target="tpu_custom_call" | custom-call | flops 200000 | bytes 100000 | tf_op jit(solution)/shard_map/added/pallas_call | solution.py:139
  9.3 17.4 %all_to_all.10.in_ref = f32[16,16,512]{2,1,0:T(8,128)S(1)} all-to-all(f32[16,16,512]{2,1,0:T(8,128)S(1)} %added.1), channel_id=1, replica_groups={{70,2,198,68,194,64,6,66,0,128,192,134,132,130,196,4},{133,199,129,7,67..., dimensions={0} | all-to-all | bytes 1048576 | tf_op jit(solution)/shard_map/all_to_all | solution.py:367
  26.7 0.6 %folded.1 = f32[8,8,128]{2,1,0:T(8,128)} custom-call(f32[16,16,512]{2,1,0:T(8,128)S(1)} %all_to_all.10.in_ref), custom_call_target="tpu_custom_call" | custom-call | flops 200000 | bytes 100000 | tf_op jit(solution)/shard_map/folded/pallas_call | solution.py:165
  27.3 15.5 %all-to-all-start.1 = ((f32[8,8,128]{2,1,0:T(8,128)}), f32[8,8,128]{2,1,0:T(8,128)S(1)}, u32[]{:S(2)}, u32[]{:S(2)}) async-start(f32[8,8,128]{2,1,0:T(8,128)} %folded.1), calls=%async_computation.1 | async-start | bytes 65536 | tf_op jit(solution)/shard_map/all_to_all | solution.py:372
  42.9 3.5 %square.1 = (f32[2,256,256]{2,1,0:T(8,128)}, f32[2,256,256]{2,1,0:T(8,128)}, f32[256,256]{1,0:T(8,128)S(1)}, bf16[2,2,256,256]{3,2,1,0:T(8,128)(2,1)S(1)}, bf16[2,256,256]{2,1,0:T(8,128)(2,1)S(1)}) custom-call(f32[2,256,256]{2,1,0:T(8,128)} %even_ref.1, f32[2,256,256]{2,1,0:T(8,128)} %inv_ref.3, f32[4,256,256]{2,1,0:T(8,128)} %link_ref.3), custom_call_target="tpu_custom_call" | custom-call | flops 800000000 | bytes 2700000 | tf_op jit(solution)/shard_map/square/pallas_call | solution.py:237
  46.4 2.9 %tall.1 = (f32[2,512,256]{2,1,0:T(8,128)}, f32[512,256]{1,0:T(8,128)S(1)}) custom-call(f32[4,512,256]{2,1,0:T(8,128)} %arrow_ref.3, bf16[2,2,256,256]{3,2,1,0:T(8,128)(2,1)S(1)} %get-tuple-element.20.left_ref, bf16[2,256,256]{2,1,0:T(8,128)(2,1)S(1)} %get-tuple-element.21.w_ref), custom_call_target="tpu_custom_call" | custom-call | flops 600000000 | bytes 2600000 | tf_op jit(solution)/shard_map/tall/pallas_call | solution.py:282
  49.3 0.0 copy-start
  49.3 0.0 collective-permute-done.got_ref
  49.3 0.9 %settle.1 = (f32[2,256,256]{2,1,0:T(8,128)}, f32[2,512,256]{2,1,0:T(8,128)}) custom-call(f32[2,256,256]{2,1,0:T(8,128)} %get-tuple-element.19.diag_ref, f32[2,512,256]{2,1,0:T(8,128)} %get-tuple-element.22.new_ref, f32[256,256]{1,0:T(8,128)S(1)} %get-tuple-element.23.square_ref, ...), custom_call_target="tpu_custom_call", output_to_operand_aliasing={{0}: (0, {}), {1}: (1, {})} | custom-call | flops 200000 | bytes 1000000 | tf_op jit(solution)/shard_map/settle/pallas_call | solution.py:314
  50.2 0.0 all-to-all-done.1.in_ref
  50.2 0.0 copy-done
  50.2 0.6 %final.1 = f32[2,512]{1,0:T(2,128)} custom-call(f32[8,8,128]{2,1,0:T(8,128)S(1)} %all-to-all-done.1.in_ref, f32[2,512]{1,0:T(2,128)S(1)} %copy-done), custom_call_target="tpu_custom_call" | custom-call | flops 10000 | bytes 40000 | tf_op jit(solution)/shard_map/final/pallas_call | solution.py:185
Async XLA Ops:
  3.9 4.6 %collective-permute-start.1 = (f32[256,512]{1,0:T(8,128)S(1)}, f32[256,512]{1,0:T(8,128)S(1)}, u32[]{:S(2)}, u32[]{:S(2)}) collective-permute-start(f32[256,512]{1,0:T(8,128)S(1)} %get-tuple-element.33), channel_id=1, source_target_pairs={{0,1},{1,0},{2,3},{3,2},{4,5},{5,4},{6,7},{7,6},{8,9},{9,8},{10,11... | collective-permute-start | bytes 1572872 | tf_op jit(solution)/shard_map/ppermute | solution.py:364
  6.1 43.2 %collective-permute-start = (f32[768,256]{1,0:T(8,128)S(1)}, f32[768,256]{1,0:T(8,128)S(1)}, u32[]{:S(2)}, u32[]{:S(2)}) collective-permute-start(f32[768,256]{1,0:T(8,128)S(1)} %get-tuple-element.28), channel_id=1, source_target_pairs={{0,1},{1,2},{2,3},{3,4},{4,5},{5,6},{6,7},{7,8},{8,9},{9,10},{10,1... | collective-permute-start | bytes 2359304 | tf_op jit(solution)/shard_map/ppermute | solution.py:354
  27.3 22.9 %all-to-all-start.1 = ((f32[8,8,128]{2,1,0:T(8,128)}), f32[8,8,128]{2,1,0:T(8,128)S(1)}, u32[]{:S(2)}, u32[]{:S(2)}) async-start(f32[8,8,128]{2,1,0:T(8,128)} %folded.1), calls=%async_computation.1 | async-start | bytes 65536 | tf_op jit(solution)/shard_map/all_to_all | solution.py:372
  49.3 1.0 %copy-start = (f32[2,512]{1,0:T(2,128)S(1)}, f32[2,512]{1,0:T(2,128)}, u32[]{:S(2)}) copy-start(f32[2,512]{1,0:T(2,128)} %tip_ref.1) | copy-start | bytes 12292

commit v3 on v2

--- a/solution.py
+++ b/solution.py
@@ -20,6 +20,7 @@
 NT = (((1,), (1,)), ((), ()))
 TN = (((0,), (0,)), ((), ()))
 HBM = pl.BlockSpec(memory_space=pltpu.HBM)
+VMEM = pl.BlockSpec(memory_space=pltpu.VMEM)
 
 
 def halves(x):
@@ -37,6 +38,12 @@
     for copy in copies:
         copy.start()
     return copies
+
+
+def send(src, dst, sem):
+    copy = pltpu.make_async_copy(src, dst, sem)
+    copy.start()
+    return copy
 
 
 def picked_rows(a_buf, h, part):
@@ -53,19 +60,26 @@
 
 
 def tip_kernel(inv_ref, arrow_ref, other_ref, a_ref, k_ref, p_ref, sems):
-    copies = start_all(
-        [pair for h in range(2) for pair in ((inv_ref.at[h], p_ref.at[h]), (arrow_ref.at[2 * h + 1], k_ref.at[h]))],
-        sems,
-    )
+    rows = k_ref.shape[1] // 2
+    pieces = [pl.ds(0, rows), pl.ds(rows, rows)]
+    pairs = []
+    for h in range(2):
+        pairs.append((inv_ref.at[h], p_ref.at[h]))
+        pairs += [(arrow_ref.at[2 * h + 1, piece], k_ref.at[h, piece]) for piece in pieces]
+    copies = start_all(pairs, sems)
     core = lax.axis_index("c")
     total = None
     for h in range(2):
-        copies[2 * h].wait()
-        copies[2 * h + 1].wait()
-        k = halves(k_ref[h])
-        a = mul(k, halves(p_ref[h]), NN)
-        a_ref[h, 0] = a[:, :128]
-        a_ref[h, 1] = a[:, 128:]
+        copies[3 * h].wait()
+        p = halves(p_ref[h])
+        parts = []
+        for i, piece in enumerate(pieces):
+            copies[3 * h + 1 + i].wait()
+            parts.append(halves(k_ref[h, piece]))
+            a = mul(parts[i], p, NN)
+            a_ref[h, 0, piece] = a[:, :128]
+            a_ref[h, 1, piece] = a[:, 128:]
+        k = tuple(jnp.concatenate(both, axis=0) for both in zip(*parts, strict=True))
         term = mul(picked_rows(a_ref, h, 1 - core), k, NT)
         total = term if total is None else total + term
     other_ref[...] = total
@@ -84,41 +98,56 @@
             jax.ShapeDtypeStruct((half, order, order), F32),
         ),
         in_specs=[HBM, HBM],
-        scratch_shapes=[pltpu.SemaphoreType.DMA((4,))],
+        scratch_shapes=[pltpu.SemaphoreType.DMA((6,))],
         cost_estimate=pl.CostEstimate(flops=800_000_000, bytes_accessed=1_600_000, transcendentals=0),
         compiler_params=pltpu.CompilerParams(vmem_limit_bytes=24 << 20),
     )(inv_odd, arrow_blocks)
 
 
-def mine_kernel(a_ref, k_ref, p_ref, link_ref, out_ref, sent_ref, v_buf, sem):
-    copy = pltpu.make_async_copy(link_ref.at[3], v_buf, sem)
-    copy.start()
+def mine_kernel(a_ref, k_ref, link_in, out_ref, link_ref, sem):
+    copy = send(link_in, link_ref, sem)
     core = lax.axis_index("c")
-    k = [halves(k_ref[h]) for h in range(2)]
-    out_ref[...] = mul(picked_rows(a_ref, 0, core), k[0], NT) + mul(picked_rows(a_ref, 1, core), k[1], NT)
+    terms = [mul(picked_rows(a_ref, h, core), halves(k_ref[h]), NT) for h in range(2)]
+    out_ref[...] = terms[0] + terms[1]
     copy.wait()
-    order = v_buf.shape[0]
-    v = halves(v_buf[...])
+
+
+def mine_part(a, k, coupling):
+    _, width, _ = k.shape
+    return pl.pallas_call(
+        mine_kernel,
+        name="mine",
+        out_shape=(
+            jax.ShapeDtypeStruct((width // 2, width), F32),
+            jax.ShapeDtypeStruct(coupling.shape, F32),
+        ),
+        in_specs=[VMEM, VMEM, HBM],
+        out_specs=[VMEM] * 2,
+        scratch_shapes=[pltpu.SemaphoreType.DMA(())],
+        cost_estimate=pl.CostEstimate(flops=400_000_000, bytes_accessed=1_500_000, transcendentals=0),
+        compiler_params=pltpu.CompilerParams(vmem_limit_bytes=24 << 20),
+    )(a, k, coupling)
+
+
+def right_kernel(k_ref, p_ref, link_ref, sent_ref):
+    order = p_ref.shape[1]
+    v = halves(link_ref[3])
     w = halves(mul(halves(p_ref[1]), v, NN))
     sent_ref[:order] = mul(v, w, TN)
-    sent_ref[order:] = mul(k[1], w, NN)
-
-
-def mine_part(a, k, p, coupling):
+    sent_ref[order:] = mul(halves(k_ref[1]), w, NN)
+
+
+def right_parts(k, p, link):
     _, width, order = k.shape
-    vmem = pl.BlockSpec(memory_space=pltpu.VMEM)
-    return pl.pallas_call(
-        mine_kernel,
-        name="mine",
-        out_shape=(
-            jax.ShapeDtypeStruct((width // 2, width), F32),
-            jax.ShapeDtypeStruct((order + width, order), F32),
-        ),
-        in_specs=[vmem, vmem, vmem, HBM],
-        scratch_shapes=[pltpu.VMEM((order, order), F32), pltpu.SemaphoreType.DMA(())],
-        cost_estimate=pl.CostEstimate(flops=800_000_000, bytes_accessed=300_000, transcendentals=0),
-        compiler_params=pltpu.CompilerParams(vmem_limit_bytes=24 << 20),
-    )(a, k, p, coupling)
+    return pl.pallas_call(
+        right_kernel,
+        name="right",
+        out_shape=jax.ShapeDtypeStruct((order + width, order), F32),
+        in_specs=[VMEM] * 3,
+        out_specs=VMEM,
+        cost_estimate=pl.CostEstimate(flops=400_000_000, bytes_accessed=100_000, transcendentals=0),
+        compiler_params=pltpu.CompilerParams(vmem_limit_bytes=24 << 20),
+    )(k, p, link)
 
 
 def add_kernel(a_ref, b_ref, out_ref, buf, sems):
@@ -191,29 +220,17 @@
     )(part, arrow_tip)
 
 
-def send(src, dst, sem):
-    copy = pltpu.make_async_copy(src, dst, sem)
-    copy.start()
-    return copy
-
-
 def square_kernel(
-    even_ref, inv_ref, link_ref, diag_ref, couple_ref, held_ref, left_ref, w_ref,
-    e_buf, p_buf, l_buf, d_out, c_out, in_sems, out_sems,
+    even_in, p_ref, link_ref, arrow_in, diag_ref, couple_ref, held_ref, left_ref, w_ref, arrow_ref,
+    even_ref, d_out, c_out, in_sems, out_sems,
 ):
-    copies = start_all(
-        [(inv_ref.at[0], p_buf.at[0]), (link_ref.at[pl.ds(0, 2)], l_buf.at[pl.ds(0, 2)])]
-        + [(inv_ref.at[1], p_buf.at[1]), (link_ref.at[pl.ds(2, 2)], l_buf.at[pl.ds(2, 2)]), (even_ref, e_buf)],
-        in_sems,
-    )
+    copies = start_all([(even_in, even_ref)] + [(arrow_in.at[2 * h], arrow_ref.at[h]) for h in range(2)], in_sems)
     outs = []
     left, u, v = [], [], []
     for h in range(2):
-        copies[2 * h].wait()
-        copies[2 * h + 1].wait()
-        p = halves(p_buf[h])
-        u.append(halves(l_buf[2 * h]))
-        v.append(halves(l_buf[2 * h + 1]))
+        p = halves(p_ref[h])
+        u.append(halves(link_ref[2 * h]))
+        v.append(halves(link_ref[2 * h + 1]))
         left.append(halves(mul(u[h], p, NN)))
         left_ref[h, 0], left_ref[h, 1] = left[h]
         c_out[h] = -mul(left[h], v[h], NN)
@@ -221,19 +238,18 @@
         if h == 0:
             w = halves(mul(p, v[0], NN))
             w_ref[0], w_ref[1] = w
-    copies[4].wait()
-    d_out[...] = e_buf[1] - mul(left[1], u[1], NT) - mul(v[0], w, TN)
+    copies[0].wait()
+    d_out[...] = even_ref[1] - mul(left[1], u[1], NT) - mul(v[0], w, TN)
     outs.append(send(d_out, diag_ref.at[1], out_sems.at[2]))
-    held_ref[...] = e_buf[0] - mul(left[0], u[0], NT)
-    for copy in outs:
+    held_ref[...] = even_ref[0] - mul(left[0], u[0], NT)
+    for copy in copies[1:] + outs:
         copy.wait()
 
 
-def square_parts(diag_even, inv_odd, coupling):
-    half, order, _ = inv_odd.shape
-    vmem = pl.BlockSpec(memory_space=pltpu.VMEM)
+def square_parts(even, p, link, arrow_blocks):
+    half, order, _ = p.shape
+    width = arrow_blocks.shape[1]
     blocks = jax.ShapeDtypeStruct((half, order, order), F32)
-    pair = pltpu.VMEM((half, order, order), F32)
     return pl.pallas_call(
         square_kernel,
         name="square",
@@ -243,60 +259,46 @@
             jax.ShapeDtypeStruct((order, order), F32),
             jax.ShapeDtypeStruct((half, 2, order, order), jnp.bfloat16),
             jax.ShapeDtypeStruct((2, order, order), jnp.bfloat16),
-        ),
-        in_specs=[HBM] * 3,
-        out_specs=[HBM, HBM, vmem, vmem, vmem],
+            jax.ShapeDtypeStruct((half, width, order), F32),
+        ),
+        in_specs=[HBM, VMEM, VMEM, HBM],
+        out_specs=[HBM, HBM] + [VMEM] * 4,
         scratch_shapes=[
-            pair,
-            pair,
-            pltpu.VMEM((2 * half, order, order), F32),
+            pltpu.VMEM((half, order, order), F32),
             pltpu.VMEM((order, order), F32),
-            pair,
-            pltpu.SemaphoreType.DMA((5,)),
+            pltpu.VMEM((half, order, order), F32),
+            pltpu.SemaphoreType.DMA((3,)),
             pltpu.SemaphoreType.DMA((3,)),
         ],
-        cost_estimate=pl.CostEstimate(flops=800_000_000, bytes_accessed=2_700_000, transcendentals=0),
-        compiler_params=pltpu.CompilerParams(vmem_limit_bytes=24 << 20),
-    )(diag_even, inv_odd, coupling)
-
-
-def tall_kernel(arrow_ref, left_ref, w_ref, new_ref, held_ref, k_buf, a_out, in_sems, out_sem):
-    frames = (3, 1, 2, 0)
-    copies = start_all([(arrow_ref.at[i], k_buf.at[i]) for i in frames], in_sems)
-    copies[0].wait()
-    later = mul(halves(k_buf[3]), (left_ref[1, 0], left_ref[1, 1]), NT)
-    copies[1].wait()
-    k = halves(k_buf[1])
-    later = later + mul(k, (w_ref[0], w_ref[1]), NN)
-    copies[2].wait()
-    a_out[...] = k_buf[2] - later
-    out = send(a_out, new_ref.at[1], out_sem)
-    copies[3].wait()
-    held_ref[...] = k_buf[0] - mul(k, (left_ref[0, 0], left_ref[0, 1]), NT)
+        cost_estimate=pl.CostEstimate(flops=800_000_000, bytes_accessed=1_700_000, transcendentals=0),
+        compiler_params=pltpu.CompilerParams(vmem_limit_bytes=24 << 20),
+    )(even, p, link, arrow_blocks)
+
+
+def tall_kernel(arrow_ref, k_ref, left_ref, w_ref, new_ref, held_ref, a_out, sem):
+    later = mul(halves(k_ref[1]), (left_ref[1, 0], left_ref[1, 1]), NT)
+    k = halves(k_ref[0])
+    a_out[...] = arrow_ref[1] - (later + mul(k, (w_ref[0], w_ref[1]), NN))
+    out = send(a_out, new_ref.at[1], sem)
+    held_ref[...] = arrow_ref[0] - mul(k, (left_ref[0, 0], left_ref[0, 1]), NT)
     out.wait()
 
 
-def tall_parts(arrow_blocks, left, w):
-    frames, width, order = arrow_blocks.shape
-    vmem = pl.BlockSpec(memory_space=pltpu.VMEM)
+def tall_parts(arrow_even, k, left, w):
+    half, width, order = k.shape
     return pl.pallas_call(
         tall_kernel,
         name="tall",
         out_shape=(
-            jax.ShapeDtypeStruct((frames // 2, width, order), F32),
+            jax.ShapeDtypeStruct((half, width, order), F32),
             jax.ShapeDtypeStruct((width, order), F32),
         ),
-        in_specs=[HBM, vmem, vmem],
-        out_specs=[HBM, vmem],
-        scratch_shapes=[
-            pltpu.VMEM((frames, width, order), F32),
-            pltpu.VMEM((width, order), F32),
-            pltpu.SemaphoreType.DMA((4,)),
-            pltpu.SemaphoreType.DMA(()),
-        ],
-        cost_estimate=pl.CostEstimate(flops=600_000_000, bytes_accessed=2_600_000, transcendentals=0),
-        compiler_params=pltpu.CompilerParams(vmem_limit_bytes=24 << 20),
-    )(arrow_blocks, left, w)
+        in_specs=[VMEM] * 4,
+        out_specs=[HBM, VMEM],
+        scratch_shapes=[pltpu.VMEM((width, order), F32), pltpu.SemaphoreType.DMA(())],
+        cost_estimate=pl.CostEstimate(flops=600_000_000, bytes_accessed=600_000, transcendentals=0),
+        compiler_params=pltpu.CompilerParams(vmem_limit_bytes=24 << 20),
+    )(arrow_even, k, left, w)
 
 
 def settle_kernel(diag_ref, new_ref, square_ref, tall_ref, got_ref, diag_out, new_out, d_buf, a_buf, sems):
@@ -318,7 +320,7 @@
             jax.ShapeDtypeStruct(diag_part.shape, F32),
             jax.ShapeDtypeStruct(arrow_part.shape, F32),
         ),
-        in_specs=[HBM] * 2 + [pl.BlockSpec(memory_space=pltpu.VMEM)] * 3,
+        in_specs=[HBM] * 2 + [VMEM] * 3,
         out_specs=[HBM] * 2,
         input_output_aliases={0: 0, 1: 1},
         scratch_shapes=[
@@ -362,12 +364,13 @@
     )
     other, a_kept, k_kept, p_kept = tip_parts(inv_odd, arrow_blocks)
     got = lax.ppermute(other, "c", [(0, 1), (1, 0)])
-    mine, sent = mine_part(a_kept, k_kept, p_kept, coupling)
+    mine, link = mine_part(a_kept, k_kept, coupling)
     part = added(mine, got, (nx * ny, own * nz, cols))
     part = lax.all_to_all(part, AXES, 0, 0, axis_index_groups=plane_groups(), tiled=True)
-    diag_part, couple_new, square, left, w = square_parts(diag_even, inv_odd, coupling)
+    sent = right_parts(k_kept, p_kept, link)
+    diag_part, couple_new, square, left, w, arrow_even = square_parts(diag_even, p_kept, link, arrow_blocks)
     received = shifted(sent, 1)
-    arrow_part, tall = tall_parts(arrow_blocks, left, w)
+    arrow_part, tall = tall_parts(arrow_even, k_kept, left, w)
     part = folded(part, own, nz)
     part = lax.all_to_all(part, AXES, 0, 0, axis_index_groups=column_groups(), tiled=True)
     tip_new = final(part, arrow_tip)

time: 51.2 us -> 50.2 us (0.980)
  Pallas kernels: 14.7 us -> 13.3 us
    pallas_call x0 -> x1, Pallas kernels: none -> 1.67 us  [right_parts(): pl.pallas_call(right_kernel, name='right', out_shape=jax.ShapeDtypeStruct...]
    pallas_call x1, Pallas kernels: 3.52 us -> 2.23 us  [square_parts(): pl.pallas_call(square_kernel, name='square', out_shape=(blocks, blocks, j...]
    pallas_call x1, Pallas kernels: 2.87 us -> 1.62 us  [tall_parts(): pl.pallas_call(tall_kernel, name='tall', out_shape=(jax.ShapeDtypeStruct(...]
  transfers between devices with their start and end apart: 3 -> 3, of which waited for: 0 -> 0; matrix products, arithmetic and copies ran while one was open for 0% -> 0% of each run, Pallas kernels for 21% -> 19%
where the time goes in v3:
time: 50.2 us; the launch traced here: 49.9 us
  starting transfers between devices  18.3 us (36%)
  blocking collectives  17.6 us (35%)
  Pallas kernels  13.3 us (26%)
  between operations  0.74 us (1%)
    all_to_all x1, blocking collectives, per_device(): lax.all_to_all(part, AXES, 0, 0, axis_index_groups=plane_groups(), tiled=...  17.6 us
    all_to_all x1, starting transfers between devices, per_device(): lax.all_to_all(part, AXES, 0, 0, axis_index_groups=column_groups(), tiled...  15.8 us
    pallas_call x1, Pallas kernels, tip_parts(): pl.pallas_call(tip_kernel, name='tip', out_shape=(jax.ShapeDtypeStruct((w...  3.17 us
    ppermute x1, starting transfers between devices, shifted(): return lax.ppermute(x, AXES, pairs)  2.39 us
    pallas_call x1, Pallas kernels, square_parts(): pl.pallas_call(square_kernel, name='square', out_shape=(blocks, blocks, j...  2.23 us
    pallas_call x1, Pallas kernels, right_parts(): pl.pallas_call(right_kernel, name='right', out_shape=jax.ShapeDtypeStruct...  1.67 us
    pallas_call x1, Pallas kernels, mine_part(): pl.pallas_call(mine_kernel, name='mine', out_shape=(jax.ShapeDtypeStruct(...  1.63 us
    pallas_call x1, Pallas kernels, tall_parts(): pl.pallas_call(tall_kernel, name='tall', out_shape=(jax.ShapeDtypeStruct(...  1.62 us
  transfers between devices with their start and end apart: 3, of which 0 were waited for; matrix products, arithmetic and copies ran while one was open for 0% of the time, Pallas kernels for 19%

profile of v3, /device:TPU:32, one launch (start us, length us, event | category | flops | bytes accessed | tf_op | source)
XLA Modules:
  0.0 49.9 jit_solution(403423549384544166)
XLA Ops:
  0.6 3.2 %tip.1 = (f32[256,512]{1,0:T(8,128)S(1)}, f32[2,2,512,128]{3,2,1,0:T(8,128)S(1)}, f32[2,512,256]{2,1,0:T(8,128)S(1)}, f32[2,256,256]{2,1,0:T(8,128)S(1)}) custom-call(f32[2,256,256]{2,1,0:T(8,128)} %inv_ref.1, f32[4,512,256]{2,1,0:T(8,128)} %arrow_in.1), custom_call_target="tpu_custom_call" | custom-call | flops 800000000 | bytes 1600000 | tf_op jit(solution)/shard_map/tip/pallas_call | solution.py:91
  3.8 0.1 collective-permute-start.1
  3.9 1.6 %mine.1 = (f32[256,512]{1,0:T(8,128)S(1)}, f32[4,256,256]{2,1,0:T(8,128)S(1)}) custom-call(f32[2,2,512,128]{3,2,1,0:T(8,128)S(1)} %get-tuple-element.21.a_ref, f32[2,512,256]{2,1,0:T(8,128)S(1)} %get-tuple-element.22.k_ref, f32[4,256,256]{2,1,0:T(8,128)} %link_in.1), custom_call_target="tpu_custom_call" | custom-call | flops 400000000 | bytes 1500000 | tf_op jit(solution)/shard_map/mine/pallas_call | solution.py:117
  5.5 1.7 %right.1 = f32[768,256]{1,0:T(8,128)} custom-call(f32[2,512,256]{2,1,0:T(8,128)S(1)} %get-tuple-element.22.k_ref, f32[2,256,256]{2,1,0:T(8,128)S(1)} %get-tuple-element.20.p_ref, f32[4,256,256]{2,1,0:T(8,128)S(1)} %get-tuple-element.23.link_ref), custom_call_target="tpu_custom_call" | custom-call | flops 400000000 | bytes 100000 | tf_op jit(solution)/shard_map/right/pallas_call | solution.py:142
  7.2 2.4 %collective-permute-start = (f32[768,256]{1,0:T(8,128)}, f32[768,256]{1,0:T(8,128)S(1)}, u32[]{:S(2)}, u32[]{:S(2)}) collective-permute-start(f32[768,256]{1,0:T(8,128)} %right.1), channel_id=1, source_target_pairs={{0,1},{1,2},{2,3},{3,4},{4,5},{5,6},{6,7},{7,8},{8,9},{9,10},{10,1... | collective-permute-start | bytes 2359304 | tf_op jit(solution)/shard_map/ppermute | solution.py:356
  9.6 0.0 collective-permute-done.1.b_ref
  9.6 0.8 %added.1 = f32[16,16,512]{2,1,0:T(8,128)S(1)} custom-call(f32[256,512]{1,0:T(8,128)S(1)} %get-tuple-element.34.a_ref, f32[256,512]{1,0:T(8,128)S(1)} %collective-permute-done.1.b_ref), custom_call_target="tpu_custom_call" | custom-call | flops 200000 | bytes 100000 | tf_op jit(solution)/shard_map/added/pallas_call | solution.py:168
  10.4 17.6 %all_to_all.10.in_ref = f32[16,16,512]{2,1,0:T(8,128)S(1)} all-to-all(f32[16,16,512]{2,1,0:T(8,128)S(1)} %added.1), channel_id=1, replica_groups={{70,2,198,68,194,64,6,66,0,128,192,134,132,130,196,4},{133,199,129,7,67..., dimensions={0} | all-to-all | bytes 1048576 | tf_op jit(solution)/shard_map/all_to_all | solution.py:369
  28.0 0.6 %folded.1 = f32[8,8,128]{2,1,0:T(8,128)} custom-call(f32[16,16,512]{2,1,0:T(8,128)S(1)} %all_to_all.10.in_ref), custom_call_target="tpu_custom_call" | custom-call | flops 200000 | bytes 100000 | tf_op jit(solution)/shard_map/folded/pallas_call | solution.py:194
  28.7 15.8 %all-to-all-start.1 = ((f32[8,8,128]{2,1,0:T(8,128)}), f32[8,8,128]{2,1,0:T(8,128)S(1)}, u32[]{:S(2)}, u32[]{:S(2)}) async-start(f32[8,8,128]{2,1,0:T(8,128)} %folded.1), calls=%async_computation.1 | async-start | bytes 65536 | tf_op jit(solution)/shard_map/all_to_all | solution.py:375
  44.5 2.2 %square.1 = (f32[2,256,256]{2,1,0:T(8,128)}, f32[2,256,256]{2,1,0:T(8,128)}, f32[256,256]{1,0:T(8,128)S(1)}, bf16[2,2,256,256]{3,2,1,0:T(8,128)(2,1)S(1)}, bf16[...) custom-call(f32[2,256,256]{2,1,0:T(8,128)} %even_in.1, f32[2,256,256]{2,1,0:T(8,128)S(1)} %get-tuple-element.20.p_ref, ...), custom_call_target="tpu_custom_call" | custom-call | flops 800000000 | bytes 1700000 | tf_op jit(solution)/shard_map/square/pallas_call | solution.py:253
  46.7 1.6 %tall.1 = (f32[2,512,256]{2,1,0:T(8,128)}, f32[512,256]{1,0:T(8,128)S(1)}) custom-call(f32[2,512,256]{2,1,0:T(8,128)S(1)} %get-tuple-element.25.arrow_ref, f32[2,512,256]{2,1,0:T(8,128)S(1)} %get-tuple-element.22.k_ref, bf16[2,2,256,256]{3,2,1,0:T(8,128)(2,1)S(1)} %get-tuple-element.26.left_ref, bf16[2,256,256]{2,1,0:T(8,128)(2,1)S(1)} %get-tuple-element.27.w_ref), custom_call_target="tpu_custom_call" | custom-call | flops 600000000 | bytes 600000 | tf_op jit(solution)/shard_map/tall/pallas_call | solution.py:289
  48.4 0.0 copy-start
  48.4 0.0 collective-permute-done.got_ref
  48.4 0.9 %settle.1 = (f32[2,256,256]{2,1,0:T(8,128)}, f32[2,512,256]{2,1,0:T(8,128)}) custom-call(f32[2,256,256]{2,1,0:T(8,128)} %get-tuple-element.24.diag_ref, f32[2,512,256]{2,1,0:T(8,128)} %get-tuple-element.28.new_ref, f32[256,256]{1,0:T(8,128)S(1)} %get-tuple-element.29.square_ref, ...), custom_call_target="tpu_custom_call", output_to_operand_aliasing={{0}: (0, {}), {1}: (1, {})} | custom-call | flops 200000 | bytes 1000000 | tf_op jit(solution)/shard_map/settle/pallas_call | solution.py:316
  49.3 0.0 all-to-all-done.1.in_ref
  49.3 0.0 copy-done
  49.3 0.6 %final.1 = f32[2,512]{1,0:T(2,128)} custom-call(f32[8,8,128]{2,1,0:T(8,128)S(1)} %all-to-all-done.1.in_ref, f32[2,512]{1,0:T(2,128)S(1)} %copy-done), custom_call_target="tpu_custom_call" | custom-call | flops 10000 | bytes 40000 | tf_op jit(solution)/shard_map/final/pallas_call | solution.py:214
Async XLA Ops:
  3.8 5.8 %collective-permute-start.1 = (f32[256,512]{1,0:T(8,128)S(1)}, f32[256,512]{1,0:T(8,128)S(1)}, u32[]{:S(2)}, u32[]{:S(2)}) collective-permute-start(f32[256,512]{1,0:T(8,128)S(1)} %get-tuple-element.35), channel_id=1, source_target_pairs={{0,1},{1,0},{2,3},{3,2},{4,5},{5,4},{6,7},{7,6},{8,9},{9,8},{10,11... | collective-permute-start | bytes 1572872 | tf_op jit(solution)/shard_map/ppermute | solution.py:366
  7.2 41.2 %collective-permute-start = (f32[768,256]{1,0:T(8,128)}, f32[768,256]{1,0:T(8,128)S(1)}, u32[]{:S(2)}, u32[]{:S(2)}) collective-permute-start(f32[768,256]{1,0:T(8,128)} %right.1), channel_id=1, source_target_pairs={{0,1},{1,2},{2,3},{3,4},{4,5},{5,6},{6,7},{7,8},{8,9},{9,10},{10,1... | collective-permute-start | bytes 2359304 | tf_op jit(solution)/shard_map/ppermute | solution.py:356
  28.7 20.7 %all-to-all-start.1 = ((f32[8,8,128]{2,1,0:T(8,128)}), f32[8,8,128]{2,1,0:T(8,128)S(1)}, u32[]{:S(2)}, u32[]{:S(2)}) async-start(f32[8,8,128]{2,1,0:T(8,128)} %folded.1), calls=%async_computation.1 | async-start | bytes 65536 | tf_op jit(solution)/shard_map/all_to_all | solution.py:375
  48.4 1.0 %copy-start = (f32[2,512]{1,0:T(2,128)S(1)}, f32[2,512]{1,0:T(2,128)}, u32[]{:S(2)}) copy-start(f32[2,512]{1,0:T(2,128)} %tip_ref.1) | copy-start | bytes 12292

commit v4 on v3

--- a/solution.py
+++ b/solution.py
@@ -46,43 +46,42 @@
     return copy
 
 
-def picked_rows(a_buf, h, part):
+def picked_rows(k_ref, h, part):
     nx, nz, ny, nc = SIZES
-    own = a_buf.shape[2] // (nx * nz * ny * nc)
+    own = k_ref.shape[2] // (nx * nz * ny * nc)
     tiles = []
     for chips in zip(*PLANE, strict=True):
         starts = [(chip // ny * nz * ny + chip % ny) * nc * own for chip in chips]
         start = jnp.where(part == 0, starts[0], starts[1]) + part * own
         for r in range(own):
             rows = pl.ds(start + r, nz, stride=ny * nc * own)
-            tiles.append(jnp.concatenate([a_buf[h, 0, rows, :], a_buf[h, 1, rows, :]], axis=1))
+            tiles.append(jnp.concatenate([k_ref[h, 0, rows, :], k_ref[h, 1, rows, :]], axis=1))
     return halves(jnp.concatenate(tiles, axis=0))
 
 
-def tip_kernel(inv_ref, arrow_ref, other_ref, a_ref, k_ref, p_ref, sems):
-    rows = k_ref.shape[1] // 2
-    pieces = [pl.ds(0, rows), pl.ds(rows, rows)]
+def whole(k_ref, h):
+    return halves(jnp.concatenate([k_ref[h, 0], k_ref[h, 1]], axis=1))
+
+
+def tip_term(k_ref, p_ref, h, part):
+    a = mul(picked_rows(k_ref, h, part), halves(p_ref[h]), NN)
+    return mul(halves(a), whole(k_ref, h), NT)
+
+
+def tip_kernel(inv_ref, arrow_ref, other_ref, k_ref, p_ref, sems):
     pairs = []
     for h in range(2):
+        frame = arrow_ref.at[2 * h + 1]
+        pairs += [(frame.at[:, pl.ds(lane * 128, 128)], k_ref.at[h, lane]) for lane in range(2)]
         pairs.append((inv_ref.at[h], p_ref.at[h]))
-        pairs += [(arrow_ref.at[2 * h + 1, piece], k_ref.at[h, piece]) for piece in pieces]
     copies = start_all(pairs, sems)
-    core = lax.axis_index("c")
-    total = None
-    for h in range(2):
-        copies[3 * h].wait()
-        p = halves(p_ref[h])
-        parts = []
-        for i, piece in enumerate(pieces):
-            copies[3 * h + 1 + i].wait()
-            parts.append(halves(k_ref[h, piece]))
-            a = mul(parts[i], p, NN)
-            a_ref[h, 0, piece] = a[:, :128]
-            a_ref[h, 1, piece] = a[:, 128:]
-        k = tuple(jnp.concatenate(both, axis=0) for both in zip(*parts, strict=True))
-        term = mul(picked_rows(a_ref, h, 1 - core), k, NT)
-        total = term if total is None else total + term
-    other_ref[...] = total
+    part = 1 - lax.axis_index("c")
+    for copy in copies[:3]:
+        copy.wait()
+    total = tip_term(k_ref, p_ref, 0, part)
+    for copy in copies[3:]:
+        copy.wait()
+    other_ref[...] = total + tip_term(k_ref, p_ref, 1, part)
 
 
 def tip_parts(inv_odd, arrow_blocks):
@@ -94,26 +93,24 @@
         out_shape=(
             jax.ShapeDtypeStruct((width // 2, width), F32),
             jax.ShapeDtypeStruct((half, 2, width, order // 2), F32),
-            jax.ShapeDtypeStruct((half, width, order), F32),
             jax.ShapeDtypeStruct((half, order, order), F32),
         ),
         in_specs=[HBM, HBM],
         scratch_shapes=[pltpu.SemaphoreType.DMA((6,))],
-        cost_estimate=pl.CostEstimate(flops=800_000_000, bytes_accessed=1_600_000, transcendentals=0),
+        cost_estimate=pl.CostEstimate(flops=600_000_000, bytes_accessed=1_600_000, transcendentals=0),
         compiler_params=pltpu.CompilerParams(vmem_limit_bytes=24 << 20),
     )(inv_odd, arrow_blocks)
 
 
-def mine_kernel(a_ref, k_ref, link_in, out_ref, link_ref, sem):
+def mine_kernel(k_ref, p_ref, link_in, out_ref, link_ref, sem):
     copy = send(link_in, link_ref, sem)
-    core = lax.axis_index("c")
-    terms = [mul(picked_rows(a_ref, h, core), halves(k_ref[h]), NT) for h in range(2)]
-    out_ref[...] = terms[0] + terms[1]
+    part = lax.axis_index("c")
+    out_ref[...] = tip_term(k_ref, p_ref, 0, part) + tip_term(k_ref, p_ref, 1, part)
     copy.wait()
 
 
-def mine_part(a, k, coupling):
-    _, width, _ = k.shape
+def mine_part(k, p, coupling):
+    width = k.shape[2]
     return pl.pallas_call(
         mine_kernel,
         name="mine",
@@ -124,25 +121,30 @@
         in_specs=[VMEM, VMEM, HBM],
         out_specs=[VMEM] * 2,
         scratch_shapes=[pltpu.SemaphoreType.DMA(())],
-        cost_estimate=pl.CostEstimate(flops=400_000_000, bytes_accessed=1_500_000, transcendentals=0),
+        cost_estimate=pl.CostEstimate(flops=600_000_000, bytes_accessed=1_100_000, transcendentals=0),
         compiler_params=pltpu.CompilerParams(vmem_limit_bytes=24 << 20),
-    )(a, k, coupling)
+    )(k, p, coupling)
 
 
 def right_kernel(k_ref, p_ref, link_ref, sent_ref):
     order = p_ref.shape[1]
+    half, quarter = order // 2, order // 4
     v = halves(link_ref[3])
     w = halves(mul(halves(p_ref[1]), v, NN))
-    sent_ref[:order] = mul(v, w, TN)
-    sent_ref[order:] = mul(halves(k_ref[1]), w, NN)
+    right, low = slice(half, order), tuple(x[:, half:] for x in v)
+    sent_ref[:half] = mul(tuple(x[:, :half] for x in v), w, TN)
+    corner = mul(low, tuple(x[:, half:] for x in w), TN)
+    sent_ref[half : half + quarter, :half] = corner[:quarter]
+    sent_ref[half : half + quarter, right] = corner[quarter:]
+    sent_ref[half + quarter :] = mul(whole(k_ref, 1), w, NN)
 
 
 def right_parts(k, p, link):
-    _, width, order = k.shape
+    width, order = k.shape[2], p.shape[1]
     return pl.pallas_call(
         right_kernel,
         name="right",
-        out_shape=jax.ShapeDtypeStruct((order + width, order), F32),
+        out_shape=jax.ShapeDtypeStruct((order * 3 // 4 + width, order), F32),
         in_specs=[VMEM] * 3,
         out_specs=VMEM,
         cost_estimate=pl.CostEstimate(flops=400_000_000, bytes_accessed=100_000, transcendentals=0),
@@ -276,8 +278,8 @@
 
 
 def tall_kernel(arrow_ref, k_ref, left_ref, w_ref, new_ref, held_ref, a_out, sem):
-    later = mul(halves(k_ref[1]), (left_ref[1, 0], left_ref[1, 1]), NT)
-    k = halves(k_ref[0])
+    later = mul(whole(k_ref, 1), (left_ref[1, 0], left_ref[1, 1]), NT)
+    k = whole(k_ref, 0)
     a_out[...] = arrow_ref[1] - (later + mul(k, (w_ref[0], w_ref[1]), NN))
     out = send(a_out, new_ref.at[1], sem)
     held_ref[...] = arrow_ref[0] - mul(k, (left_ref[0, 0], left_ref[0, 1]), NT)
@@ -285,7 +287,7 @@
 
 
 def tall_parts(arrow_even, k, left, w):
-    half, width, order = k.shape
+    half, width, order = arrow_even.shape
     return pl.pallas_call(
         tall_kernel,
         name="tall",
@@ -301,15 +303,30 @@
     )(arrow_even, k, left, w)
 
 
-def settle_kernel(diag_ref, new_ref, square_ref, tall_ref, got_ref, diag_out, new_out, d_buf, a_buf, sems):
+def settle_kernel(diag_ref, new_ref, square_ref, tall_ref, got_in, diag_out, new_out, d_buf, a_buf, g_buf, in_sems, sems):
     del diag_ref, new_ref
-    order = got_ref.shape[1]
-    d_buf[...] = square_ref[...] - got_ref[:order]
-    first = send(d_buf, diag_out.at[0], sems.at[0])
-    a_buf[...] = tall_ref[...] - got_ref[order:]
-    second = send(a_buf, new_out.at[0], sems.at[1])
-    first.wait()
-    second.wait()
+    order = got_in.shape[1]
+    half, quarter = order // 2, order // 4
+    head, width = half + quarter, a_buf.shape[0]
+    rows = width // 2
+    cuts = [pl.ds(0, head), pl.ds(head, rows), pl.ds(head + rows, rows)]
+    copies = start_all([(got_in.at[cut], g_buf.at[cut]) for cut in cuts], in_sems)
+    outs = []
+    copies[0].wait()
+    top = g_buf[:half]
+    d_buf[:half] = square_ref[:half] - top
+    d_buf[half:, :half] = square_ref[half:, :half] - top[:, half:].T
+    d_buf[half:head, half:] = square_ref[half:head, half:] - g_buf[half:head, :half]
+    d_buf[head:, half:] = square_ref[head:, half:] - g_buf[half:head, half:]
+    outs.append(send(d_buf, diag_out.at[0], sems.at[0]))
+    for i in range(2):
+        copies[1 + i].wait()
+        here = slice(i * rows, (i + 1) * rows)
+        a_buf[here] = tall_ref[here] - g_buf[head + i * rows : head + (i + 1) * rows]
+        part = pl.ds(i * rows, rows)
+        outs.append(send(a_buf.at[part], new_out.at[0, part], sems.at[1 + i]))
+    for copy in outs:
+        copy.wait()
 
 
 def settle(diag_part, arrow_part, square, tall, received):
@@ -320,15 +337,17 @@
             jax.ShapeDtypeStruct(diag_part.shape, F32),
             jax.ShapeDtypeStruct(arrow_part.shape, F32),
         ),
-        in_specs=[HBM] * 2 + [VMEM] * 3,
+        in_specs=[HBM, HBM, VMEM, VMEM, HBM],
         out_specs=[HBM] * 2,
         input_output_aliases={0: 0, 1: 1},
         scratch_shapes=[
             pltpu.VMEM(square.shape, F32),
             pltpu.VMEM(tall.shape, F32),
-            pltpu.SemaphoreType.DMA((2,)),
+            pltpu.VMEM(received.shape, F32),
+            pltpu.SemaphoreType.DMA((3,)),
+            pltpu.SemaphoreType.DMA((3,)),
         ],
-        cost_estimate=pl.CostEstimate(flops=200_000, bytes_accessed=1_000_000, transcendentals=0),
+        cost_estimate=pl.CostEstimate(flops=200_000, bytes_accessed=1_500_000, transcendentals=0),
         compiler_params=pltpu.CompilerParams(vmem_limit_bytes=16 << 20),
     )(diag_part, arrow_part, square, tall, received)
 
@@ -362,9 +381,9 @@
     diag_even, inv_odd, coupling, arrow_blocks = (
         pltpu.with_memory_space_constraint(x, pltpu.HBM) for x in (diag_even, inv_odd, coupling, arrow_blocks)
     )
-    other, a_kept, k_kept, p_kept = tip_parts(inv_odd, arrow_blocks)
+    other, k_kept, p_kept = tip_parts(inv_odd, arrow_blocks)
     got = lax.ppermute(other, "c", [(0, 1), (1, 0)])
-    mine, link = mine_part(a_kept, k_kept, coupling)
+    mine, link = mine_part(k_kept, p_kept, coupling)
     part = added(mine, got, (nx * ny, own * nz, cols))
     part = lax.all_to_all(part, AXES, 0, 0, axis_index_groups=plane_groups(), tiled=True)
     sent = right_parts(k_kept, p_kept, link)

time: 50.2 us -> 48.9 us (0.974)
  blocking collectives: 17.6 us -> 16.9 us
    all_to_all x1, blocking collectives: 17.6 us -> 16.9 us  [per_device(): lax.all_to_all(part, AXES, 0, 0, axis_index_groups=plane_groups(), tiled=...]
    pallas_call x1, Pallas kernels: 3.17 us -> 2.65 us  [tip_parts(): pl.pallas_call(tip_kernel, name='tip', out_shape=(jax.ShapeDtypeStruct((w...]
  transfers between devices with their start and end apart: 3 -> 3, of which waited for: 0 -> 0; matrix products, arithmetic and copies ran while one was open for 0% -> 0% of each run, Pallas kernels for 19% -> 20%
where the time goes in v4:
time: 48.9 us; the launch traced here: 48.7 us
  starting transfers between devices  18.2 us (37%)
  blocking collectives  16.9 us (35%)
  Pallas kernels  12.8 us (26%)
  between operations  0.74 us (2%)
    all_to_all x1, blocking collectives, per_device(): lax.all_to_all(part, AXES, 0, 0, axis_index_groups=plane_groups(), tiled=...  16.9 us
    all_to_all x1, starting transfers between devices, per_device(): lax.all_to_all(part, AXES, 0, 0, axis_index_groups=column_groups(), tiled...  15.7 us
    pallas_call x1, Pallas kernels, tip_parts(): pl.pallas_call(tip_kernel, name='tip', out_shape=(jax.ShapeDtypeStruct((w...  2.65 us
    ppermute x1, starting transfers between devices, shifted(): return lax.ppermute(x, AXES, pairs)  2.39 us
    pallas_call x1, Pallas kernels, square_parts(): pl.pallas_call(square_kernel, name='square', out_shape=(blocks, blocks, j...  2.23 us
    pallas_call x1, Pallas kernels, right_parts(): pl.pallas_call(right_kernel, name='right', out_shape=jax.ShapeDtypeStruct...  1.66 us
    pallas_call x1, Pallas kernels, tall_parts(): pl.pallas_call(tall_kernel, name='tall', out_shape=(jax.ShapeDtypeStruct(...  1.62 us
    pallas_call x1, Pallas kernels, mine_part(): pl.pallas_call(mine_kernel, name='mine', out_shape=(jax.ShapeDtypeStruct(...  1.33 us
  transfers between devices with their start and end apart: 3, of which 0 were waited for; matrix products, arithmetic and copies ran while one was open for 0% of the time, Pallas kernels for 20%

profile of v4, /device:TPU:32, one launch (start us, length us, event | category | flops | bytes accessed | tf_op | source)
XLA Modules:
  0.0 48.7 jit_solution(709861537856603836)
XLA Ops:
  0.6 2.7 %tip.1 = (f32[256,512]{1,0:T(8,128)S(1)}, f32[2,2,512,128]{3,2,1,0:T(8,128)S(1)}, f32[2,256,256]{2,1,0:T(8,128)S(1)}) custom-call(f32[2,256,256]{2,1,0:T(8,128)} %inv_ref.1, f32[4,512,256]{2,1,0:T(8,128)} %arrow_in.1), custom_call_target="tpu_custom_call" | custom-call | flops 600000000 | bytes 1600000 | tf_op jit(solution)/shard_map/tip/pallas_call | solution.py:90
  3.3 0.1 collective-permute-start.1
  3.4 1.3 %mine.1 = (f32[256,512]{1,0:T(8,128)S(1)}, f32[4,256,256]{2,1,0:T(8,128)S(1)}) custom-call(f32[2,2,512,128]{3,2,1,0:T(8,128)S(1)} %get-tuple-element.20.k_ref, f32[2,256,256]{2,1,0:T(8,128)S(1)} %get-tuple-element.19.p_ref, f32[4,256,256]{2,1,0:T(8,128)} %link_in.1), custom_call_target="tpu_custom_call" | custom-call | flops 600000000 | bytes 1100000 | tf_op jit(solution)/shard_map/mine/pallas_call | solution.py:114
  4.7 1.7 %right.1 = f32[704,256]{1,0:T(8,128)} custom-call(f32[2,2,512,128]{3,2,1,0:T(8,128)S(1)} %get-tuple-element.20.k_ref, f32[2,256,256]{2,1,0:T(8,128)S(1)} %get-tuple-element.19.p_ref, f32[4,256,256]{2,1,0:T(8,128)S(1)} %get-tuple-element.21.link_ref), custom_call_target="tpu_custom_call" | custom-call | flops 400000000 | bytes 100000 | tf_op jit(solution)/shard_map/right/pallas_call | solution.py:144
  6.4 2.4 %collective-permute-start = (f32[704,256]{1,0:T(8,128)}, f32[704,256]{1,0:T(8,128)S(1)}, u32[]{:S(2)}, u32[]{:S(2)}) collective-permute-start(f32[704,256]{1,0:T(8,128)} %right.1), channel_id=1, source_target_pairs={{0,1},{1,2},{2,3},{3,4},{4,5},{5,6},{6,7},{7,8},{8,9},{9,10},{10,1... | collective-permute-start | bytes 2162696 | tf_op jit(solution)/shard_map/ppermute | solution.py:375
  8.8 0.0 collective-permute-done.1.b_ref
  8.8 0.8 %added.1 = f32[16,16,512]{2,1,0:T(8,128)S(1)} custom-call(f32[256,512]{1,0:T(8,128)S(1)} %get-tuple-element.32.a_ref, f32[256,512]{1,0:T(8,128)S(1)} %collective-permute-done.1.b_ref), custom_call_target="tpu_custom_call" | custom-call | flops 200000 | bytes 100000 | tf_op jit(solution)/shard_map/added/pallas_call | solution.py:170
  9.6 16.9 %all_to_all.10.in_ref = f32[16,16,512]{2,1,0:T(8,128)S(1)} all-to-all(f32[16,16,512]{2,1,0:T(8,128)S(1)} %added.1), channel_id=1, replica_groups={{70,2,198,68,194,64,6,66,0,128,192,134,132,130,196,4},{133,199,129,7,67..., dimensions={0} | all-to-all | bytes 1048576 | tf_op jit(solution)/shard_map/all_to_all | solution.py:388
  26.5 0.6 %folded.1 = f32[8,8,128]{2,1,0:T(8,128)} custom-call(f32[16,16,512]{2,1,0:T(8,128)S(1)} %all_to_all.10.in_ref), custom_call_target="tpu_custom_call" | custom-call | flops 200000 | bytes 100000 | tf_op jit(solution)/shard_map/folded/pallas_call | solution.py:196
  27.1 15.7 %all-to-all-start.1 = ((f32[8,8,128]{2,1,0:T(8,128)}), f32[8,8,128]{2,1,0:T(8,128)S(1)}, u32[]{:S(2)}, u32[]{:S(2)}) async-start(f32[8,8,128]{2,1,0:T(8,128)} %folded.1), calls=%async_computation.1 | async-start | bytes 65536 | tf_op jit(solution)/shard_map/all_to_all | solution.py:394
  42.8 2.2 %square.1 = (f32[2,256,256]{2,1,0:T(8,128)}, f32[2,256,256]{2,1,0:T(8,128)}, f32[256,256]{1,0:T(8,128)S(1)}, bf16[2,2,256,256]{3,2,1,0:T(8,128)(2,1)S(1)}, bf16[...) custom-call(f32[2,256,256]{2,1,0:T(8,128)} %even_in.1, f32[2,256,256]{2,1,0:T(8,128)S(1)} %get-tuple-element.19.p_ref, ...), custom_call_target="tpu_custom_call" | custom-call | flops 800000000 | bytes 1700000 | tf_op jit(solution)/shard_map/square/pallas_call | solution.py:255
  45.1 1.6 %tall.1 = (f32[2,512,256]{2,1,0:T(8,128)}, f32[512,256]{1,0:T(8,128)S(1)}) custom-call(f32[2,512,256]{2,1,0:T(8,128)S(1)} %get-tuple-element.23.arrow_ref, f32[2,2,512,128]{3,2,1,0:T(8,128)S(1)} %get-tuple-element.20.k_ref, bf16[2,2,256,256]{3,2,1,0:T(8,128)(2,1)S(1)} %get-tuple-element.24.left_ref, bf16[2,256,256]{2,1,0:T(8,128)(2,1)S(1)} %get-tuple-element.25.w_ref), custom_call_target="tpu_custom_call" | custom-call | flops 600000000 | bytes 600000 | tf_op jit(solution)/shard_map/tall/pallas_call | solution.py:291
  46.7 0.0 copy-start
  46.7 0.0 collective-permute-done.got_in
  46.7 1.3 %settle.1 = (f32[2,256,256]{2,1,0:T(8,128)}, f32[2,512,256]{2,1,0:T(8,128)}) custom-call(f32[2,256,256]{2,1,0:T(8,128)} %get-tuple-element.22.diag_ref, f32[2,512,256]{2,1,0:T(8,128)} %get-tuple-element.26.new_ref, f32[256,256]{1,0:T(8,128)S(1)} %get-tuple-element.27.square_ref, ...), custom_call_target="tpu_custom_call", output_to_operand_aliasing={{0}: (0, {}), {1}: (1, {})} | custom-call | flops 200000 | bytes 1500000 | tf_op jit(solution)/shard_map/settle/pallas_call | solution.py:333
  48.0 0.0 all-to-all-done.1.in_ref
  48.0 0.0 copy-done
  48.1 0.6 %final.1 = f32[2,512]{1,0:T(2,128)} custom-call(f32[8,8,128]{2,1,0:T(8,128)S(1)} %all-to-all-done.1.in_ref, f32[2,512]{1,0:T(2,128)S(1)} %copy-done), custom_call_target="tpu_custom_call" | custom-call | flops 10000 | bytes 40000 | tf_op jit(solution)/shard_map/final/pallas_call | solution.py:216
Async XLA Ops:
  3.3 5.5 %collective-permute-start.1 = (f32[256,512]{1,0:T(8,128)S(1)}, f32[256,512]{1,0:T(8,128)S(1)}, u32[]{:S(2)}, u32[]{:S(2)}) collective-permute-start(f32[256,512]{1,0:T(8,128)S(1)} %get-tuple-element.33), channel_id=1, source_target_pairs={{0,1},{1,0},{2,3},{3,2},{4,5},{5,4},{6,7},{7,6},{8,9},{9,8},{10,11... | collective-permute-start | bytes 1572872 | tf_op jit(solution)/shard_map/ppermute | solution.py:385
  6.4 40.3 %collective-permute-start = (f32[704,256]{1,0:T(8,128)}, f32[704,256]{1,0:T(8,128)S(1)}, u32[]{:S(2)}, u32[]{:S(2)}) collective-permute-start(f32[704,256]{1,0:T(8,128)} %right.1), channel_id=1, source_target_pairs={{0,1},{1,2},{2,3},{3,4},{4,5},{5,6},{6,7},{7,8},{8,9},{9,10},{10,1... | collective-permute-start | bytes 2162696 | tf_op jit(solution)/shard_map/ppermute | solution.py:375
  27.1 20.9 %all-to-all-start.1 = ((f32[8,8,128]{2,1,0:T(8,128)}), f32[8,8,128]{2,1,0:T(8,128)S(1)}, u32[]{:S(2)}, u32[]{:S(2)}) async-start(f32[8,8,128]{2,1,0:T(8,128)} %folded.1), calls=%async_computation.1 | async-start | bytes 65536 | tf_op jit(solution)/shard_map/all_to_all | solution.py:394
  46.7 1.4 %copy-start = (f32[2,512]{1,0:T(2,128)S(1)}, f32[2,512]{1,0:T(2,128)}, u32[]{:S(2)}) copy-start(f32[2,512]{1,0:T(2,128)} %tip_ref.1) | copy-start | bytes 12292

commit v5 on v4

--- a/solution.py
+++ b/solution.py
@@ -11,10 +11,10 @@
 AXES = ("x", "z", "y", "c")
 SIZES = (4, 8, 4, 2)
 PLANE = (
-    (7, 1, 15, 6, 13, 4, 3, 5, 0, 8, 12, 11, 10, 9, 14, 2),
-    (10, 15, 8, 3, 5, 14, 4, 9, 13, 1, 0, 2, 7, 6, 11, 12),
+    (14, 1, 3, 15, 8, 0, 7, 9, 6, 4, 13, 5, 11, 2, 12, 10),
+    (10, 6, 4, 9, 15, 12, 2, 11, 14, 7, 1, 13, 8, 0, 5, 3),
 )
-COLUMN = (4, 0, 2, 6, 1, 5, 3, 7)
+COLUMN = (4, 0, 1, 7, 2, 6, 3, 5)
 F32 = jnp.float32
 NN = (((1,), (0,)), ((), ()))
 NT = (((1,), (1,)), ((), ()))

time: 48.9 us -> 48.3 us (0.988)
  starting transfers between devices: 18.2 us -> 17.5 us
    all_to_all x1, starting transfers between devices: 15.7 us -> 15 us  [per_device(): lax.all_to_all(part, AXES, 0, 0, axis_index_groups=column_groups(), tiled...]
where the time goes in v5:
time: 48.3 us; the launch traced here: 48 us
  starting transfers between devices  17.5 us (36%)
  blocking collectives  17 us (35%)
  Pallas kernels  12.8 us (27%)
  between operations  0.74 us (2%)
    all_to_all x1, blocking collectives, per_device(): lax.all_to_all(part, AXES, 0, 0, axis_index_groups=plane_groups(), tiled=...  17 us
    all_to_all x1, starting transfers between devices, per_device(): lax.all_to_all(part, AXES, 0, 0, axis_index_groups=column_groups(), tiled...  15 us
    pallas_call x1, Pallas kernels, tip_parts(): pl.pallas_call(tip_kernel, name='tip', out_shape=(jax.ShapeDtypeStruct((w...  2.65 us
    ppermute x1, starting transfers between devices, shifted(): return lax.ppermute(x, AXES, pairs)  2.4 us
    pallas_call x1, Pallas kernels, square_parts(): pl.pallas_call(square_kernel, name='square', out_shape=(blocks, blocks, j...  2.23 us
    pallas_call x1, Pallas kernels, right_parts(): pl.pallas_call(right_kernel, name='right', out_shape=jax.ShapeDtypeStruct...  1.66 us
    pallas_call x1, Pallas kernels, tall_parts(): pl.pallas_call(tall_kernel, name='tall', out_shape=(jax.ShapeDtypeStruct(...  1.62 us
    pallas_call x1, Pallas kernels, mine_part(): pl.pallas_call(mine_kernel, name='mine', out_shape=(jax.ShapeDtypeStruct(...  1.34 us
  transfers between devices with their start and end apart: 3, of which 0 were waited for; matrix products, arithmetic and copies ran while one was open for 0% of the time, Pallas kernels for 20%

profile of v5, /device:TPU:32, one launch (start us, length us, event | category | flops | bytes accessed | tf_op | source)
XLA Modules:
  0.0 48.0 jit_solution(13057212141091664067)
XLA Ops:
  0.6 2.6 %tip.1 = (f32[256,512]{1,0:T(8,128)S(1)}, f32[2,2,512,128]{3,2,1,0:T(8,128)S(1)}, f32[2,256,256]{2,1,0:T(8,128)S(1)}) custom-call(f32[2,256,256]{2,1,0:T(8,128)} %inv_ref.1, f32[4,512,256]{2,1,0:T(8,128)} %arrow_in.1), custom_call_target="tpu_custom_call" | custom-call | flops 600000000 | bytes 1600000 | tf_op jit(solution)/shard_map/tip/pallas_call | solution.py:90
  3.3 0.1 collective-permute-start.1
  3.4 1.3 %mine.1 = (f32[256,512]{1,0:T(8,128)S(1)}, f32[4,256,256]{2,1,0:T(8,128)S(1)}) custom-call(f32[2,2,512,128]{3,2,1,0:T(8,128)S(1)} %get-tuple-element.20.k_ref, f32[2,256,256]{2,1,0:T(8,128)S(1)} %get-tuple-element.19.p_ref, f32[4,256,256]{2,1,0:T(8,128)} %link_in.1), custom_call_target="tpu_custom_call" | custom-call | flops 600000000 | bytes 1100000 | tf_op jit(solution)/shard_map/mine/pallas_call | solution.py:114
  4.7 1.7 %right.1 = f32[704,256]{1,0:T(8,128)} custom-call(f32[2,2,512,128]{3,2,1,0:T(8,128)S(1)} %get-tuple-element.20.k_ref, f32[2,256,256]{2,1,0:T(8,128)S(1)} %get-tuple-element.19.p_ref, f32[4,256,256]{2,1,0:T(8,128)S(1)} %get-tuple-element.21.link_ref), custom_call_target="tpu_custom_call" | custom-call | flops 400000000 | bytes 100000 | tf_op jit(solution)/shard_map/right/pallas_call | solution.py:144
  6.4 2.4 %collective-permute-start = (f32[704,256]{1,0:T(8,128)}, f32[704,256]{1,0:T(8,128)S(1)}, u32[]{:S(2)}, u32[]{:S(2)}) collective-permute-start(f32[704,256]{1,0:T(8,128)} %right.1), channel_id=1, source_target_pairs={{0,1},{1,2},{2,3},{3,4},{4,5},{5,6},{6,7},{7,8},{8,9},{9,10},{10,1... | collective-permute-start | bytes 2162696 | tf_op jit(solution)/shard_map/ppermute | solution.py:375
  8.8 0.0 collective-permute-done.1.b_ref
  8.8 0.8 %added.1 = f32[16,16,512]{2,1,0:T(8,128)S(1)} custom-call(f32[256,512]{1,0:T(8,128)S(1)} %get-tuple-element.32.a_ref, f32[256,512]{1,0:T(8,128)S(1)} %collective-permute-done.1.b_ref), custom_call_target="tpu_custom_call" | custom-call | flops 200000 | bytes 100000 | tf_op jit(solution)/shard_map/added/pallas_call | solution.py:170
  9.6 17.0 %all_to_all.10.in_ref = f32[16,16,512]{2,1,0:T(8,128)S(1)} all-to-all(f32[16,16,512]{2,1,0:T(8,128)S(1)} %added.1), channel_id=1, replica_groups={{196,2,6,198,128,0,70,130,68,64,194,66,134,4,192,132},{133,69,65,131,19..., dimensions={0} | all-to-all | bytes 1048576 | tf_op jit(solution)/shard_map/all_to_all | solution.py:388
  26.6 0.6 %folded.1 = f32[8,8,128]{2,1,0:T(8,128)} custom-call(f32[16,16,512]{2,1,0:T(8,128)S(1)} %all_to_all.10.in_ref), custom_call_target="tpu_custom_call" | custom-call | flops 200000 | bytes 100000 | tf_op jit(solution)/shard_map/folded/pallas_call | solution.py:196
  27.2 15.0 %all-to-all-start.1 = ((f32[8,8,128]{2,1,0:T(8,128)}), f32[8,8,128]{2,1,0:T(8,128)S(1)}, u32[]{:S(2)}, u32[]{:S(2)}) async-start(f32[8,8,128]{2,1,0:T(8,128)} %folded.1), calls=%async_computation.1 | async-start | bytes 65536 | tf_op jit(solution)/shard_map/all_to_all | solution.py:394
  42.2 2.2 %square.1 = (f32[2,256,256]{2,1,0:T(8,128)}, f32[2,256,256]{2,1,0:T(8,128)}, f32[256,256]{1,0:T(8,128)S(1)}, bf16[2,2,256,256]{3,2,1,0:T(8,128)(2,1)S(1)}, bf16[...) custom-call(f32[2,256,256]{2,1,0:T(8,128)} %even_in.1, f32[2,256,256]{2,1,0:T(8,128)S(1)} %get-tuple-element.19.p_ref, ...), custom_call_target="tpu_custom_call" | custom-call | flops 800000000 | bytes 1700000 | tf_op jit(solution)/shard_map/square/pallas_call | solution.py:255
  44.4 1.6 %tall.1 = (f32[2,512,256]{2,1,0:T(8,128)}, f32[512,256]{1,0:T(8,128)S(1)}) custom-call(f32[2,512,256]{2,1,0:T(8,128)S(1)} %get-tuple-element.23.arrow_ref, f32[2,2,512,128]{3,2,1,0:T(8,128)S(1)} %get-tuple-element.20.k_ref, bf16[2,2,256,256]{3,2,1,0:T(8,128)(2,1)S(1)} %get-tuple-element.24.left_ref, bf16[2,256,256]{2,1,0:T(8,128)(2,1)S(1)} %get-tuple-element.25.w_ref), custom_call_target="tpu_custom_call" | custom-call | flops 600000000 | bytes 600000 | tf_op jit(solution)/shard_map/tall/pallas_call | solution.py:291
  46.0 0.0 copy-start
  46.1 0.0 collective-permute-done.got_in
  46.1 1.3 %settle.1 = (f32[2,256,256]{2,1,0:T(8,128)}, f32[2,512,256]{2,1,0:T(8,128)}) custom-call(f32[2,256,256]{2,1,0:T(8,128)} %get-tuple-element.22.diag_ref, f32[2,512,256]{2,1,0:T(8,128)} %get-tuple-element.26.new_ref, f32[256,256]{1,0:T(8,128)S(1)} %get-tuple-element.27.square_ref, ...), custom_call_target="tpu_custom_call", output_to_operand_aliasing={{0}: (0, {}), {1}: (1, {})} | custom-call | flops 200000 | bytes 1500000 | tf_op jit(solution)/shard_map/settle/pallas_call | solution.py:333
  47.4 0.0 all-to-all-done.1.in_ref
  47.4 0.0 copy-done
  47.4 0.6 %final.1 = f32[2,512]{1,0:T(2,128)} custom-call(f32[8,8,128]{2,1,0:T(8,128)S(1)} %all-to-all-done.1.in_ref, f32[2,512]{1,0:T(2,128)S(1)} %copy-done), custom_call_target="tpu_custom_call" | custom-call | flops 10000 | bytes 40000 | tf_op jit(solution)/shard_map/final/pallas_call | solution.py:216
Async XLA Ops:
  3.3 5.5 %collective-permute-start.1 = (f32[256,512]{1,0:T(8,128)S(1)}, f32[256,512]{1,0:T(8,128)S(1)}, u32[]{:S(2)}, u32[]{:S(2)}) collective-permute-start(f32[256,512]{1,0:T(8,128)S(1)} %get-tuple-element.33), channel_id=1, source_target_pairs={{0,1},{1,0},{2,3},{3,2},{4,5},{5,4},{6,7},{7,6},{8,9},{9,8},{10,11... | collective-permute-start | bytes 1572872 | tf_op jit(solution)/shard_map/ppermute | solution.py:385
  6.4 39.7 %collective-permute-start = (f32[704,256]{1,0:T(8,128)}, f32[704,256]{1,0:T(8,128)S(1)}, u32[]{:S(2)}, u32[]{:S(2)}) collective-permute-start(f32[704,256]{1,0:T(8,128)} %right.1), channel_id=1, source_target_pairs={{0,1},{1,2},{2,3},{3,4},{4,5},{5,6},{6,7},{7,8},{8,9},{9,10},{10,1... | collective-permute-start | bytes 2162696 | tf_op jit(solution)/shard_map/ppermute | solution.py:375
  27.2 20.2 %all-to-all-start.1 = ((f32[8,8,128]{2,1,0:T(8,128)}), f32[8,8,128]{2,1,0:T(8,128)S(1)}, u32[]{:S(2)}, u32[]{:S(2)}) async-start(f32[8,8,128]{2,1,0:T(8,128)} %folded.1), calls=%async_computation.1 | async-start | bytes 65536 | tf_op jit(solution)/shard_map/all_to_all | solution.py:394
  46.0 1.4 %copy-start = (f32[2,512]{1,0:T(2,128)S(1)}, f32[2,512]{1,0:T(2,128)}, u32[]{:S(2)}) copy-start(f32[2,512]{1,0:T(2,128)} %tip_ref.1) | copy-start | bytes 12292
